TPU v7x, 256 devices: a whole 4x4x8 slice. The times are simulated.
256 devices in a mesh: gx: 16 (over y_lo, x, core), ch: 16 (over z, y_hi).
Axes of the slice: x: 4, y: 4 (y_hi: 2, y_lo: 2; y = y_hi * 2 + y_lo), z: 8, core: 2. Of those that a mesh axis runs over, the one named last changes fastest.
Arguments:
- activations: bfloat16 [128, 256, 4, 128], P('ch', 'gx'), may hold values from -6 to 6
- conv_weight: bfloat16 [27, 128, 128], P(None, None, 'ch'), may hold values from -0.109375 to 0.109375
- out_grad: bfloat16 [128, 256, 4, 128], P('ch', 'gx'), may hold values from -6 to 6
Outputs:
- features_out: bfloat16 [128, 256, 4, 128], P('ch', 'gx')
- input_grad: bfloat16 [128, 256, 4, 128], P('ch', 'gx')
All inputs are finite; a program needn't handle non-finite values.
Results may differ from a plain program's by a relative error of at most 0.001.
Values may be sent and summed in bfloat16 or wider, within the bound.
No kernel may reach another device: no remote copies, remote signals or barrier semaphores. Data moves between devices by JAX's collectives and lax.ppermute only.
A program may use at most 64 MiB of HBM per device.

v0:
```python
import functools

import jax
import jax.numpy as jnp
from jax import lax
from jax.experimental import pallas as pl
from jax.experimental.pallas import tpu as pltpu
from jax.sharding import PartitionSpec as P


VMEM = pl.BlockSpec(memory_space=pltpu.VMEM)
HBM = pl.BlockSpec(memory_space=pltpu.HBM)
PARAMS = pltpu.CompilerParams(vmem_limit_bytes=16 * 2**20)
F32 = jnp.float32
BF16 = jnp.bfloat16


def lanes(shape):
    return lax.broadcasted_iota(jnp.int32, shape, len(shape) - 1)


def pair_of(level, core, count):
    return level + core * (count // 2 - 1 - 2 * level)


def pieces(taps):
    return (0, taps // 2), (taps + 3) // 4


def places_of(slab):
    core, x, y = lax.rem(slab, 2), lax.rem(slab // 2, 2), slab // 8
    return core, y + core * (x - y), x + core * (y - x)


def both(first, second):
    size = first.shape[-1]
    early = lanes(first.shape) < size // 2
    turned_first, turned_second = (pltpu.roll(x, size // 2, x.ndim - 1) for x in (first, second))
    return jnp.where(early, first, turned_second), jnp.where(early, turned_first, second)


def pack_kernel(act_hbm, grad_hbm, weight_hbm, send_ref, act_ref, grad_ref, weight_ref, rows_ref, sems):
    copies = [
        pltpu.make_async_copy(source, target, sems.at[at])
        for at, (source, target) in enumerate(
            ((act_hbm, act_ref), (grad_hbm, grad_ref), (weight_hbm, weight_ref))
        )
    ]
    for copy in copies:
        copy.start()
    core = lax.rem(lax.axis_index("gx"), 2)
    count, (rows, _, depth, height) = send_ref.shape[0], act_ref.shape
    taps, _, fan = weight_ref.shape
    block = rows * depth
    side = height // 2
    copies[0].wait()
    copies[1].wait()
    lane = lanes((rows, height))
    for level in range(count // 2):
        pair = pair_of(level, core, count)
        edges = [jnp.zeros((rows, height), F32) for _ in range(2)]
        for plane in range(2):
            maps = []
            for tensor, ref in enumerate((act_ref, grad_ref)):
                values = ref[:, 2 * pair + plane].reshape(block, height).astype(F32)
                maps.append(values)
                rows_ref[...] = values
                for z in range(depth):
                    column = rows_ref[pl.ds(z, rows, stride=depth), :]
                    spot = side * plane + 8 * tensor + z
                    for half in range(2):
                        edge = side - half
                        turned = pltpu.roll(column, (spot - edge) % height, 1)
                        edges[half] = jnp.where(lane == spot, turned, edges[half])
            start = plane * (block + rows)
            for half, values in enumerate(both(*maps)):
                send_ref[2 * level + half, start : start + block, :] = values.astype(BF16)
        for half in range(2):
            send_ref[2 * level + half, block : block + rows, :] = edges[half].astype(BF16)
    copies[2].wait()
    _, place, _ = places_of(lax.axis_index("gx"))
    (_, second), size = pieces(taps)
    filters = weight_ref[pl.ds(core * second + place * size, size)].reshape(size * rows, fan)
    for chip in range(count):
        send_ref[chip, 2 * block + rows :, :] = filters


def prepare_kernel(own_ref, core_ref, near_ref, diagonal_ref, forward_ref, backward_ref, filters_ref, *, taps):
    count, _, channels = own_ref.shape
    rows = channels // count
    core, place, other = places_of(lax.axis_index("gx"))
    (_, second), size = pieces(taps)
    filters_ref[2 * core + place] = own_ref[...]
    filters_ref[2 * core + 1 - place] = near_ref[...]
    filters_ref[2 - 2 * core + other] = core_ref[...]
    filters_ref[3 - 2 * core - other] = diagonal_ref[...]

    def spot(index):
        return slice(index * channels, (index + 1) * channels)

    for a in range(3):
        for b in range(3):
            for c in range(3):
                tap = 9 * a + 3 * b + c
                half = 0 if tap < 2 * size else 1
                part, at = divmod(tap - half * second, size)
                matrix = filters_ref[2 * half + part, :, at * rows : (at + 1) * rows, :].reshape(channels, channels)
                forward_ref[spot(b), spot(3 * c + a)] = matrix
                backward_ref[spot(b), spot(3 * c + a)] = matrix.T


def conv_kernel(own_ref, low_ref, high_ref, forward_ref, backward_ref, send_ref,
                forward_cells_ref, backward_cells_ref, wide_ref, *, depth):
    count, span, height = own_ref.shape
    rows = span // (2 * depth + 1)
    block = rows * depth
    channels = count * rows
    side = height // 2
    right = lax.rem(lax.axis_index("ch"), 2)
    cells_refs = (forward_cells_ref, backward_cells_ref)

    def spot(index):
        return slice(index * channels, (index + 1) * channels)

    lane = lanes((channels, height))
    early = lane < side
    within = lane % side

    def edge_of(ref, start):
        return ref[:, start : start + rows, :].astype(F32).reshape(channels, height)

    own_edge, low_edge, high_edge = edge_of(own_ref, block), edge_of(low_ref, 0), edge_of(high_ref, block)
    edges = (
        pltpu.roll(jnp.where(early, own_edge, low_edge), side, 1),
        own_edge,
        pltpu.roll(jnp.where(early, high_edge, own_edge), side, 1),
    )
    planes = (
        low_ref[:, rows : rows + block, :],
        own_ref[:, 0:block, :],
        own_ref[:, block + rows : 2 * block + rows, :],
        high_ref[:, 0:block, :],
    )
    for at, values in enumerate(planes):
        wide_ref[at] = values.astype(F32).reshape(channels * depth, height)

    for c in range(3):
        for tensor in range(2):
            direction = 1 - 2 * tensor
            outside = 0 if direction * (c - 1) < 0 else depth - 1
            if c != 1:
                cells_refs[tensor][3 * c * channels : 3 * (c + 1) * channels, outside * height : (outside + 1) * height] = (
                    jnp.zeros((3 * channels, height), BF16)
                )
            for a in range(3):
                edge = edges[1 + direction * (a - 1)]
                shift = 8 * tensor + direction * (c - 1)
                source = within + direction * (c - 1)
                inside = (within < depth) & (source >= 0) & (source < depth)
                moved = pltpu.roll(edge, -shift % height, 1)
                cells_refs[tensor][spot(3 * c + a), depth * height :] = jnp.where(inside, moved, 0.0).astype(BF16)
    for z in range(depth):
        pieces = [wide_ref[at, pl.ds(z, channels, stride=depth), :] for at in range(4)]
        for step in range(3):
            for tensor, values in enumerate(both_planes(pieces[step], pieces[step + 1], early, side)):
                direction = 1 - 2 * tensor
                a = 1 + direction * (step - 1)
                values = values.astype(BF16)
                for c in range(3):
                    target = z - direction * (c - 1)
                    if 0 <= target < depth:
                        cells_refs[tensor][spot(3 * c + a), target * height : (target + 1) * height] = values

    for tensor in range(2):
        direction = 1 - 2 * tensor
        filters_ref = (forward_ref, backward_ref)[tensor]
        sums = jnp.dot(filters_ref[...], cells_refs[tensor][:, : depth * height], preferred_element_type=F32)
        b = pl.multiple_of((1 + direction - 2 * direction * right) * channels, channels)
        beyond = jnp.dot(filters_ref[pl.ds(b, channels), :], cells_refs[tensor][:, depth * height :],
                         preferred_element_type=F32)
        border = jnp.where(right == 1, 0, side - 1)
        for z in range(depth):
            columns = slice(z * height, (z + 1) * height)
            before, middle, after = (sums[spot(b), columns] for b in (1 - direction, 1, 1 + direction))
            before = jnp.where(within == 0, 0.0, pltpu.roll(before, 1, 1))
            after = jnp.where(within == side - 1, 0.0, pltpu.roll(after, height - 1, 1))
            extra = jnp.where(within == border, pltpu.roll(beyond, border + (height - z), 1), 0.0)
            wide_ref[tensor, pl.ds(z, channels, stride=depth), :] = before + middle + after + extra
        result = wide_ref[tensor].astype(BF16).reshape(count, block, height)
        send_ref[:, tensor * block : (tensor + 1) * block, :] = result


def both_planes(first, second, early, side):
    turned_first, turned_second = pltpu.roll(first, side, 1), pltpu.roll(second, side, 1)
    return jnp.where(early, first, turned_second), jnp.where(early, turned_first, second)


def unpack_kernel(got_ref, features_ref, gradient_ref):
    core = lax.rem(lax.axis_index("gx"), 2)
    count, _, height = got_ref.shape
    rows, _, depth, _ = features_ref.shape
    block = rows * depth
    for level in range(count // 2):
        pair = pair_of(level, core, count)
        for tensor, ref in enumerate((features_ref, gradient_ref)):
            start = tensor * block
            halves = [got_ref[2 * level + side, start : start + block, :].astype(F32) for side in range(2)]
            for plane, values in enumerate(both(*halves)):
                ref[:, 2 * pair + plane] = values.astype(BF16).reshape(rows, depth, height)


def local(slabs, count, activations, conv_weight, out_grad):
    rows, _, depth, height = activations.shape
    taps, channels, _ = conv_weight.shape
    block = rows * depth
    span = 2 * block + rows
    shared = pieces(taps)[1] * rows
    pairs = count // 2
    send = pl.pallas_call(
        pack_kernel,
        out_shape=jax.ShapeDtypeStruct((count, span + shared, height), BF16),
        in_specs=[HBM, HBM, HBM],
        out_specs=VMEM,
        scratch_shapes=[
            pltpu.VMEM(activations.shape, BF16),
            pltpu.VMEM(out_grad.shape, BF16),
            pltpu.VMEM((taps, rows, channels), BF16),
            pltpu.VMEM((block, height), F32),
            pltpu.SemaphoreType.DMA((3,)),
        ],
        compiler_params=PARAMS,
        name="pack",
    )(*(pltpu.with_memory_space_constraint(x, pltpu.HBM) for x in (activations, out_grad, jnp.swapaxes(conv_weight, 1, 2))))
    got = lax.all_to_all(send, "ch", 0, 0, tiled=True)
    own, own_filters = got[:, :span], got[:, span:]
    across_core = [(slab, slab ^ 1) for slab in range(slabs)]
    across = [(slab, slab ^ (2 if slab % 2 else 8)) for slab in range(slabs)]
    near_filters = lax.ppermute(own_filters, "gx", across)
    core_filters = lax.ppermute(own_filters, "gx", across_core)
    diagonal_filters = lax.ppermute(near_filters, "gx", across_core)
    ring = []
    for side in range(2):
        order = [
            slab * count + 2 * pair_of(pair, slab % 2, count) + side for slab in range(slabs) for pair in range(pairs)
        ]
        ring += zip(order, order[1:] + order[:1])
    low = lax.ppermute(got[:, block:span], ("gx", "ch"), ring)
    high = lax.ppermute(got[:, : block + rows], ("gx", "ch"), [(to, at) for at, to in ring])
    forward, backward = pl.pallas_call(
        functools.partial(prepare_kernel, taps=taps),
        out_shape=[jax.ShapeDtypeStruct((3 * channels, 9 * channels), BF16)] * 2,
        in_specs=[VMEM] * 4,
        out_specs=[VMEM, VMEM],
        scratch_shapes=[pltpu.VMEM((4, count, shared, channels), BF16)],
        cost_estimate=pl.CostEstimate(flops=0, bytes_accessed=4 * 2**20, transcendentals=0),
        compiler_params=PARAMS,
        name="prepare",
    )(own_filters, core_filters, near_filters, diagonal_filters)
    result = pl.pallas_call(
        functools.partial(conv_kernel, depth=depth),
        out_shape=jax.ShapeDtypeStruct((count, 2 * block, height), BF16),
        in_specs=[VMEM, VMEM, VMEM, VMEM, VMEM],
        out_specs=VMEM,
        scratch_shapes=[
            pltpu.VMEM((9 * channels, (depth + 1) * height), BF16),
            pltpu.VMEM((9 * channels, (depth + 1) * height), BF16),
            pltpu.VMEM((4, channels * depth, height), F32),
        ],
        compiler_params=PARAMS,
        name="conv",
    )(own, low, high, forward, backward)
    back = lax.all_to_all(result, "ch", 0, 0, tiled=True)
    return pl.pallas_call(
        unpack_kernel,
        out_shape=(jax.ShapeDtypeStruct(activations.shape, BF16), jax.ShapeDtypeStruct(out_grad.shape, BF16)),
        in_specs=[VMEM],
        out_specs=(VMEM, VMEM),
        compiler_params=PARAMS,
        name="unpack",
    )(back)


def solution(mesh):
    return jax.shard_map(
        functools.partial(local, mesh.shape["gx"], mesh.shape["ch"]),
        mesh=mesh,
        in_specs=(P("ch", "gx", None, None), P(None, None, "ch"), P("ch", "gx", None, None)),
        out_specs=(P("ch", "gx", None, None), P("ch", "gx", None, None)),
        check_vma=False,
    )
```

profile of v0, /device:TPU:2, one launch (start us, length us, event | category | flops | bytes accessed | tf_op | source)
XLA Modules:
  0.0 65.5 jit_solution(14079287374497320409)
XLA Ops:
  0.6 1.4 %pack.1 = bf16[16,128,128]{2,1,0:T(8,128)(2,1)S(1)} custom-call(bf16[8,16,4,128]{3,2,1,0:T(4,128)(2,1)} %act_hbm.1, bf16[8,16,4,128]{3,2,1,0:T(4,128)(2,1)} %grad_hbm.1, bf16[27,8,128]{2,1,0:T(8,128)(2,1)} %bitcast.1), custom_call_target="tpu_custom_call" | custom-call | tf_op jit(solution)/shard_map/pack/pallas_call | solution.py:219
  2.0 29.8 %all_to_all.10 = bf16[16,128,128]{2,1,0:T(8,128)(2,1)S(1)} all-to-all(bf16[16,128,128]{2,1,0:T(8,128)(2,1)S(1)} %pack.1), channel_id=1, replica_groups=mesh['gx'=16,'ch'=16] {'ch'}, dimensions={0} | all-to-all | bytes 1048576 | tf_op jit(solution)/shard_map/all_to_all | solution.py:234
  31.9 0.8 %collective-permute-start.3 = (bf16[16,56,128]{2,1,0:T(8,128)(2,1)S(1)}, bf16[16,56,128]{2,1,0:T(8,128)(2,1)S(1)}, u32[]{:S(2)}, u32[]{:S(2)}) collective-permute-start(bf16[16,56,128]{2,1,0:T(8,128)(2,1)S(1)} %slice.19.own_ref), channel_id=1, source_target_pairs={{0,128},{16,48},{32,160},{48,16},{64,192},{80,112},{96,224},{112,8... | collective-permute-start | bytes 688136 | tf_op jit(solution)/shard_map/ppermute | solution.py:238
  32.6 0.0 collective-permute-start.2
  32.6 5.3 %collective-permute-done.3.near_ref = bf16[16,56,128]{2,1,0:T(8,128)(2,1)S(1)} collective-permute-done((bf16[16,56,128]{2,1,0:T(8,128)(2,1)S(1)}, bf16[16,56,128]{2,1,0:T(8,128)(2,1)S(1)}, u32[]{:S(2)}, u32[]{:S(2)}) %collective-permute-start.3) | collective-permute-done | bytes 229408 | tf_op jit(solution)/shard_map/ppermute | solution.py:238
  38.0 0.0 collective-permute-start.4
  38.0 0.1 collective-permute-start
  38.1 1.7 %collective-permute-start.1 = (bf16[16,40,128]{2,1,0:T(8,128)(2,1)S(1)}, bf16[16,40,128]{2,1,0:T(8,128)(2,1)S(1)}, u32[]{:S(2)}, u32[]{:S(2)}) collective-permute-start(bf16[16,40,128]{2,1,0:T(8,128)(2,1)S(1)} %get-tuple-element.6), channel_id=1, source_target_pairs={{2,0},{4,2},{6,4},{8,6},{10,8},{12,10},{14,12},{30,14},{28,30},{26... | collective-permute-start | bytes 491528 | tf_op jit(solution)/shard_map/ppermute | solution.py:248
  39.9 0.0 collective-permute-done.2.core_ref
  39.9 0.0 collective-permute-done.4.diagonal_ref
  39.9 0.4 prepare.1
  40.4 2.5 %collective-permute-done.low_ref = bf16[16,40,128]{2,1,0:T(8,128)(2,1)S(1)} collective-permute-done((bf16[16,40,128]{2,1,0:T(8,128)(2,1)S(1)}, bf16[16,40,128]{2,1,0:T(8,128)(2,1)S(1)}, u32[]{:S(2)}, u32[]{:S(2)}) %collective-permute-start) | collective-permute-done | bytes 163872 | tf_op jit(solution)/shard_map/ppermute | solution.py:247
  42.9 1.9 %collective-permute-done.1.high_ref = bf16[16,40,128]{2,1,0:T(8,128)(2,1)S(1)} collective-permute-done((bf16[16,40,128]{2,1,0:T(8,128)(2,1)S(1)}, bf16[16,40,128]{2,1,0:T(8,128)(2,1)S(1)}, u32[]{:S(2)}, u32[]{:S(2)}) %collective-permute-start.1) | collective-permute-done | bytes 163872 | tf_op jit(solution)/shard_map/ppermute | solution.py:248
  44.7 1.8 %conv.1 = bf16[16,64,128]{2,1,0:T(8,128)(2,1)S(1)} custom-call(bf16[16,72,128]{2,1,0:T(8,128)(2,1)S(1)} %slice.16.own_ref, bf16[16,40,128]{2,1,0:T(8,128)(2,1)S(1)} %collective-permute-done.low_ref, bf16[16,40,128]{2,1,0:T(8,128)(2,1)S(1)} %collective-permute-done.1.high_ref, bf16[384,1152]{1,0:T(8,128)(2,1)S(1)} %get-tuple-element.4.forward_ref, ...), custom_call_target="tpu_custom_call" | custom-call | tf_op jit(solution)/shard_map/conv/pallas_call | solution.py:259
  46.5 18.1 %all_to_all.11.got_ref = bf16[16,64,128]{2,1,0:T(8,128)(2,1)S(1)} all-to-all(bf16[16,64,128]{2,1,0:T(8,128)(2,1)S(1)} %conv.1), channel_id=1, replica_groups=mesh['gx'=16,'ch'=16] {'ch'}, dimensions={0} | all-to-all | bytes 524288 | tf_op jit(solution)/shard_map/all_to_all | solution.py:272
  64.6 0.9 %unpack.1 = (bf16[8,16,4,128]{3,2,1,0:T(4,128)(2,1)}, bf16[8,16,4,128]{3,2,1,0:T(4,128)(2,1)}) custom-call(bf16[16,64,128]{2,1,0:T(8,128)(2,1)S(1)} %all_to_all.11.got_ref), custom_call_target="tpu_custom_call" | custom-call | tf_op jit(solution)/shard_map/unpack/pallas_call | solution.py:273
  (3 shorter events, 0.1 us)
Async XLA Ops:
  31.9 6.1 %collective-permute-start.3 = (bf16[16,56,128]{2,1,0:T(8,128)(2,1)S(1)}, bf16[16,56,128]{2,1,0:T(8,128)(2,1)S(1)}, u32[]{:S(2)}, u32[]{:S(2)}) collective-permute-start(bf16[16,56,128]{2,1,0:T(8,128)(2,1)S(1)} %slice.19.own_ref), channel_id=1, source_target_pairs={{0,128},{16,48},{32,160},{48,16},{64,192},{80,112},{96,224},{112,8... | collective-permute-start | bytes 688136 | tf_op jit(solution)/shard_map/ppermute | solution.py:238
  32.6 7.2 %collective-permute-start.2 = (bf16[16,56,128]{2,1,0:T(8,128)(2,1)S(1)}, bf16[16,56,128]{2,1,0:T(8,128)(2,1)S(1)}, u32[]{:S(2)}, u32[]{:S(2)}) collective-permute-start(bf16[16,56,128]{2,1,0:T(8,128)(2,1)S(1)} %slice.19.own_ref), channel_id=1, source_target_pairs={{0,16},{16,0},{32,48},{48,32},{64,80},{80,64},{96,112},{112,96},{1... | collective-permute-start | bytes 688136 | tf_op jit(solution)/shard_map/ppermute | solution.py:239
  38.0 1.9 %collective-permute-start.4 = (bf16[16,56,128]{2,1,0:T(8,128)(2,1)S(1)}, bf16[16,56,128]{2,1,0:T(8,128)(2,1)S(1)}, u32[]{:S(2)}, u32[]{:S(2)}) collective-permute-start(bf16[16,56,128]{2,1,0:T(8,128)(2,1)S(1)} %collective-permute-done.3.near_ref), channel_id=1, source_target_pairs={{0,16},{16,0},{32,48},{48,32},{64,80},{80,64},{96,112},{112,96},{1... | collective-permute-start | bytes 688136 | tf_op jit(solution)/shard_map/ppermute | solution.py:240
  38.0 4.8 %collective-permute-start = (bf16[16,40,128]{2,1,0:T(8,128)(2,1)S(1)}, bf16[16,40,128]{2,1,0:T(8,128)(2,1)S(1)}, u32[]{:S(2)}, u32[]{:S(2)}) collective-permute-start(bf16[16,40,128]{2,1,0:T(8,128)(2,1)S(1)} %get-tuple-element.7), channel_id=1, source_target_pairs={{0,2},{2,4},{4,6},{6,8},{8,10},{10,12},{12,14},{14,30},{30,28},{28... | collective-permute-start | bytes 491528 | tf_op jit(solution)/shard_map/ppermute | solution.py:247
  38.1 6.6 %collective-permute-start.1 = (bf16[16,40,128]{2,1,0:T(8,128)(2,1)S(1)}, bf16[16,40,128]{2,1,0:T(8,128)(2,1)S(1)}, u32[]{:S(2)}, u32[]{:S(2)}) collective-permute-start(bf16[16,40,128]{2,1,0:T(8,128)(2,1)S(1)} %get-tuple-element.6), channel_id=1, source_target_pairs={{2,0},{4,2},{6,4},{8,6},{10,8},{12,10},{14,12},{30,14},{28,30},{26... | collective-permute-start | bytes 491528 | tf_op jit(solution)/shard_map/ppermute | solution.py:248
where the time goes:
time: 65.7 us; the launch traced here: 65.5 us
  blocking collectives  47.9 us (73%)
  waiting for transfers between devices  9.71 us (15%)
  Pallas kernels  4.52 us (7%)
  starting transfers between devices  2.6 us (4%)
  between operations  0.69 us (1%)
    all_to_all x1, blocking collectives, local(): got = lax.all_to_all(send, 'ch', 0, 0, tiled=True)  29.8 us
    all_to_all x1, blocking collectives, local(): back = lax.all_to_all(result, 'ch', 0, 0, tiled=True)  18.1 us
    ppermute x1, waiting for transfers between devices, local(): near_filters = lax.ppermute(own_filters, 'gx', across)  5.34 us
    ppermute x1, waiting for transfers between devices, local(): low = lax.ppermute(got[:, block:span], ('gx', 'ch'), ring)  2.5 us
    ppermute x1, waiting for transfers between devices, local(): lax.ppermute(got[:, :block + rows], ('gx', 'ch'), [(to, at) for at, to in...  1.87 us
    pallas_call x1, Pallas kernels, local(): pl.pallas_call(functools.partial(conv_kernel, depth=depth), out_shape=jax...  1.79 us
    ppermute x1, starting transfers between devices, local(): lax.ppermute(got[:, :block + rows], ('gx', 'ch'), [(to, at) for at, to in...  1.73 us
    pallas_call x1, Pallas kernels, local(): pl.pallas_call(pack_kernel, out_shape=jax.ShapeDtypeStruct((count, span +...  1.4 us
  transfers between devices with their start and end apart: 5, of which 3 were waited for; matrix products, arithmetic and copies ran while one was open for 0% of the time, Pallas kernels for 1%

commit v1 on v0

--- a/solution.py
+++ b/solution.py
@@ -5,12 +5,13 @@
 from jax import lax
 from jax.experimental import pallas as pl
 from jax.experimental.pallas import tpu as pltpu
-from jax.sharding import PartitionSpec as P
+from jax.sharding import Mesh, PartitionSpec as P
 
 
 VMEM = pl.BlockSpec(memory_space=pltpu.VMEM)
 HBM = pl.BlockSpec(memory_space=pltpu.HBM)
 PARAMS = pltpu.CompilerParams(vmem_limit_bytes=16 * 2**20)
+CH = ("level", "side")
 F32 = jnp.float32
 BF16 = jnp.bfloat16
 
@@ -30,6 +31,10 @@
 def places_of(slab):
     core, x, y = lax.rem(slab, 2), lax.rem(slab // 2, 2), slab // 8
     return core, y + core * (x - y), x + core * (y - x)
+
+
+def turned(chip, count):
+    return chip % 2 * (count // 2) + chip // 2
 
 
 def both(first, second):
@@ -116,7 +121,7 @@
     block = rows * depth
     channels = count * rows
     side = height // 2
-    right = lax.rem(lax.axis_index("ch"), 2)
+    right = lax.axis_index("side")
     cells_refs = (forward_cells_ref, backward_cells_ref)
 
     def spot(index):
@@ -186,8 +191,9 @@
             after = jnp.where(within == side - 1, 0.0, pltpu.roll(after, height - 1, 1))
             extra = jnp.where(within == border, pltpu.roll(beyond, border + (height - z), 1), 0.0)
             wide_ref[tensor, pl.ds(z, channels, stride=depth), :] = before + middle + after + extra
-        result = wide_ref[tensor].astype(BF16).reshape(count, block, height)
-        send_ref[:, tensor * block : (tensor + 1) * block, :] = result
+        for chip in range(count):
+            result = wide_ref[tensor, chip * block : (chip + 1) * block, :].astype(BF16)
+            send_ref[turned(chip, count), tensor * block : (tensor + 1) * block, :] = result
 
 
 def both_planes(first, second, early, side):
@@ -204,7 +210,7 @@
         pair = pair_of(level, core, count)
         for tensor, ref in enumerate((features_ref, gradient_ref)):
             start = tensor * block
-            halves = [got_ref[2 * level + side, start : start + block, :].astype(F32) for side in range(2)]
+            halves = [got_ref[turned(2 * level + side, count), start : start + block, :].astype(F32) for side in range(2)]
             for plane, values in enumerate(both(*halves)):
                 ref[:, 2 * pair + plane] = values.astype(BF16).reshape(rows, depth, height)
 
@@ -231,7 +237,7 @@
         compiler_params=PARAMS,
         name="pack",
     )(*(pltpu.with_memory_space_constraint(x, pltpu.HBM) for x in (activations, out_grad, jnp.swapaxes(conv_weight, 1, 2))))
-    got = lax.all_to_all(send, "ch", 0, 0, tiled=True)
+    got = lax.all_to_all(send, CH, 0, 0, tiled=True)
     own, own_filters = got[:, :span], got[:, span:]
     across_core = [(slab, slab ^ 1) for slab in range(slabs)]
     across = [(slab, slab ^ (2 if slab % 2 else 8)) for slab in range(slabs)]
@@ -244,8 +250,8 @@
             slab * count + 2 * pair_of(pair, slab % 2, count) + side for slab in range(slabs) for pair in range(pairs)
         ]
         ring += zip(order, order[1:] + order[:1])
-    low = lax.ppermute(got[:, block:span], ("gx", "ch"), ring)
-    high = lax.ppermute(got[:, : block + rows], ("gx", "ch"), [(to, at) for at, to in ring])
+    low = lax.ppermute(got[:, block:span], ("gx", *CH), ring)
+    high = lax.ppermute(got[:, : block + rows], ("gx", *CH), [(to, at) for at, to in ring])
     forward, backward = pl.pallas_call(
         functools.partial(prepare_kernel, taps=taps),
         out_shape=[jax.ShapeDtypeStruct((3 * channels, 9 * channels), BF16)] * 2,
@@ -269,7 +275,7 @@
         compiler_params=PARAMS,
         name="conv",
     )(own, low, high, forward, backward)
-    back = lax.all_to_all(result, "ch", 0, 0, tiled=True)
+    back = lax.all_to_all(result, CH[::-1], 0, 0, tiled=True)
     return pl.pallas_call(
         unpack_kernel,
         out_shape=(jax.ShapeDtypeStruct(activations.shape, BF16), jax.ShapeDtypeStruct(out_grad.shape, BF16)),
@@ -281,10 +287,12 @@
 
 
 def solution(mesh):
+    slabs, count = mesh.shape["gx"], mesh.shape["ch"]
+    mesh = Mesh(mesh.devices.reshape(slabs, count // 2, 2), ("gx", *CH))
     return jax.shard_map(
-        functools.partial(local, mesh.shape["gx"], mesh.shape["ch"]),
+        functools.partial(local, slabs, count),
         mesh=mesh,
-        in_specs=(P("ch", "gx", None, None), P(None, None, "ch"), P("ch", "gx", None, None)),
-        out_specs=(P("ch", "gx", None, None), P("ch", "gx", None, None)),
+        in_specs=(P(CH, "gx", None, None), P(None, None, CH), P(CH, "gx", None, None)),
+        out_specs=(P(CH, "gx", None, None), P(CH, "gx", None, None)),
         check_vma=False,
     )

time: 65.7 us -> 63.7 us (0.970)
  blocking collectives: 47.9 us -> 45.9 us
    all_to_all x2, blocking collectives: 47.9 us -> 45.9 us  [the longest x1 29.8 us: local(): got = lax.all_to_all(send, CH, 0, 0, tiled=True)]
where the time goes in v1:
time: 63.7 us; the launch traced here: 63.5 us
  blocking collectives  45.9 us (72%)
  waiting for transfers between devices  9.71 us (15%)
  Pallas kernels  4.52 us (7%)
  starting transfers between devices  2.6 us (4%)
  between operations  0.69 us (1%)
    all_to_all x1, blocking collectives, local(): got = lax.all_to_all(send, CH, 0, 0, tiled=True)  29.8 us
    all_to_all x1, blocking collectives, local(): back = lax.all_to_all(result, CH[::-1], 0, 0, tiled=True)  16.1 us
    ppermute x1, waiting for transfers between devices, local(): near_filters = lax.ppermute(own_filters, 'gx', across)  5.34 us
    ppermute x1, waiting for transfers between devices, local(): low = lax.ppermute(got[:, block:span], ('gx', *CH), ring)  2.5 us
    ppermute x1, waiting for transfers between devices, local(): lax.ppermute(got[:, :block + rows], ('gx', *CH), [(to, at) for at, to in...  1.87 us
    pallas_call x1, Pallas kernels, local(): pl.pallas_call(functools.partial(conv_kernel, depth=depth), out_shape=jax...  1.79 us
    ppermute x1, starting transfers between devices, local(): lax.ppermute(got[:, :block + rows], ('gx', *CH), [(to, at) for at, to in...  1.73 us
    pallas_call x1, Pallas kernels, local(): pl.pallas_call(pack_kernel, out_shape=jax.ShapeDtypeStruct((count, span +...  1.4 us
  transfers between devices with their start and end apart: 5, of which 3 were waited for; matrix products, arithmetic and copies ran while one was open for 0% of the time, Pallas kernels for 1%

profile of v1, /device:TPU:2, one launch (start us, length us, event | category | flops | bytes accessed | tf_op | source)
XLA Modules:
  0.0 63.5 jit_solution(8977820121706718998)
XLA Ops:
  0.6 1.4 %pack.1 = bf16[16,128,128]{2,1,0:T(8,128)(2,1)S(1)} custom-call(bf16[8,16,4,128]{3,2,1,0:T(4,128)(2,1)} %act_hbm.1, bf16[8,16,4,128]{3,2,1,0:T(4,128)(2,1)} %grad_hbm.1, bf16[27,8,128]{2,1,0:T(8,128)(2,1)} %bitcast.1), custom_call_target="tpu_custom_call" | custom-call | tf_op jit(solution)/shard_map/pack/pallas_call | solution.py:225
  2.0 29.8 %all_to_all.10 = bf16[16,128,128]{2,1,0:T(8,128)(2,1)S(1)} all-to-all(bf16[16,128,128]{2,1,0:T(8,128)(2,1)S(1)} %pack.1), channel_id=1, replica_groups=mesh['gx'=16,'level'=8,'side'=2] {'level','side'}, dimensions={0} | all-to-all | bytes 1048576 | tf_op jit(solution)/shard_map/all_to_all | solution.py:240
  31.9 0.8 %collective-permute-start.3 = (bf16[16,56,128]{2,1,0:T(8,128)(2,1)S(1)}, bf16[16,56,128]{2,1,0:T(8,128)(2,1)S(1)}, u32[]{:S(2)}, u32[]{:S(2)}) collective-permute-start(bf16[16,56,128]{2,1,0:T(8,128)(2,1)S(1)} %slice.19.own_ref), channel_id=1, source_target_pairs={{0,128},{16,48},{32,160},{48,16},{64,192},{80,112},{96,224},{112,8... | collective-permute-start | bytes 688136 | tf_op jit(solution)/shard_map/ppermute | solution.py:244
  32.6 0.0 collective-permute-start.2
  32.6 5.3 %collective-permute-done.3.near_ref = bf16[16,56,128]{2,1,0:T(8,128)(2,1)S(1)} collective-permute-done((bf16[16,56,128]{2,1,0:T(8,128)(2,1)S(1)}, bf16[16,56,128]{2,1,0:T(8,128)(2,1)S(1)}, u32[]{:S(2)}, u32[]{:S(2)}) %collective-permute-start.3) | collective-permute-done | bytes 229408 | tf_op jit(solution)/shard_map/ppermute | solution.py:244
  38.0 0.0 collective-permute-start.4
  38.0 0.1 collective-permute-start
  38.1 1.7 %collective-permute-start.1 = (bf16[16,40,128]{2,1,0:T(8,128)(2,1)S(1)}, bf16[16,40,128]{2,1,0:T(8,128)(2,1)S(1)}, u32[]{:S(2)}, u32[]{:S(2)}) collective-permute-start(bf16[16,40,128]{2,1,0:T(8,128)(2,1)S(1)} %get-tuple-element.6), channel_id=1, source_target_pairs={{2,0},{4,2},{6,4},{8,6},{10,8},{12,10},{14,12},{30,14},{28,30},{26... | collective-permute-start | bytes 491528 | tf_op jit(solution)/shard_map/ppermute | solution.py:254
  39.9 0.0 collective-permute-done.2.core_ref
  39.9 0.0 collective-permute-done.4.diagonal_ref
  39.9 0.4 prepare.1
  40.4 2.5 %collective-permute-done.low_ref = bf16[16,40,128]{2,1,0:T(8,128)(2,1)S(1)} collective-permute-done((bf16[16,40,128]{2,1,0:T(8,128)(2,1)S(1)}, bf16[16,40,128]{2,1,0:T(8,128)(2,1)S(1)}, u32[]{:S(2)}, u32[]{:S(2)}) %collective-permute-start) | collective-permute-done | bytes 163872 | tf_op jit(solution)/shard_map/ppermute | solution.py:253
  42.9 1.9 %collective-permute-done.1.high_ref = bf16[16,40,128]{2,1,0:T(8,128)(2,1)S(1)} collective-permute-done((bf16[16,40,128]{2,1,0:T(8,128)(2,1)S(1)}, bf16[16,40,128]{2,1,0:T(8,128)(2,1)S(1)}, u32[]{:S(2)}, u32[]{:S(2)}) %collective-permute-start.1) | collective-permute-done | bytes 163872 | tf_op jit(solution)/shard_map/ppermute | solution.py:254
  44.7 1.8 %conv.1 = bf16[16,64,128]{2,1,0:T(8,128)(2,1)S(1)} custom-call(bf16[16,72,128]{2,1,0:T(8,128)(2,1)S(1)} %slice.16.own_ref, bf16[16,40,128]{2,1,0:T(8,128)(2,1)S(1)} %collective-permute-done.low_ref, bf16[16,40,128]{2,1,0:T(8,128)(2,1)S(1)} %collective-permute-done.1.high_ref, bf16[384,1152]{1,0:T(8,128)(2,1)S(1)} %get-tuple-element.4.forward_ref, ...), custom_call_target="tpu_custom_call" | custom-call | tf_op jit(solution)/shard_map/conv/pallas_call | solution.py:265
  46.5 16.1 %all_to_all.11.got_ref = bf16[16,64,128]{2,1,0:T(8,128)(2,1)S(1)} all-to-all(bf16[16,64,128]{2,1,0:T(8,128)(2,1)S(1)} %conv.1), channel_id=1, replica_groups=mesh['gx'=16,'level'=8,'side'=2] {'side','level'}, dimensions={0} | all-to-all | bytes 524288 | tf_op jit(solution)/shard_map/all_to_all | solution.py:278
  62.6 0.9 %unpack.1 = (bf16[8,16,4,128]{3,2,1,0:T(4,128)(2,1)}, bf16[8,16,4,128]{3,2,1,0:T(4,128)(2,1)}) custom-call(bf16[16,64,128]{2,1,0:T(8,128)(2,1)S(1)} %all_to_all.11.got_ref), custom_call_target="tpu_custom_call" | custom-call | tf_op jit(solution)/shard_map/unpack/pallas_call | solution.py:279
  (3 shorter events, 0.1 us)
Async XLA Ops:
  31.9 6.1 %collective-permute-start.3 = (bf16[16,56,128]{2,1,0:T(8,128)(2,1)S(1)}, bf16[16,56,128]{2,1,0:T(8,128)(2,1)S(1)}, u32[]{:S(2)}, u32[]{:S(2)}) collective-permute-start(bf16[16,56,128]{2,1,0:T(8,128)(2,1)S(1)} %slice.19.own_ref), channel_id=1, source_target_pairs={{0,128},{16,48},{32,160},{48,16},{64,192},{80,112},{96,224},{112,8... | collective-permute-start | bytes 688136 | tf_op jit(solution)/shard_map/ppermute | solution.py:244
  32.6 7.2 %collective-permute-start.2 = (bf16[16,56,128]{2,1,0:T(8,128)(2,1)S(1)}, bf16[16,56,128]{2,1,0:T(8,128)(2,1)S(1)}, u32[]{:S(2)}, u32[]{:S(2)}) collective-permute-start(bf16[16,56,128]{2,1,0:T(8,128)(2,1)S(1)} %slice.19.own_ref), channel_id=1, source_target_pairs={{0,16},{16,0},{32,48},{48,32},{64,80},{80,64},{96,112},{112,96},{1... | collective-permute-start | bytes 688136 | tf_op jit(solution)/shard_map/ppermute | solution.py:245
  38.0 1.9 %collective-permute-start.4 = (bf16[16,56,128]{2,1,0:T(8,128)(2,1)S(1)}, bf16[16,56,128]{2,1,0:T(8,128)(2,1)S(1)}, u32[]{:S(2)}, u32[]{:S(2)}) collective-permute-start(bf16[16,56,128]{2,1,0:T(8,128)(2,1)S(1)} %collective-permute-done.3.near_ref), channel_id=1, source_target_pairs={{0,16},{16,0},{32,48},{48,32},{64,80},{80,64},{96,112},{112,96},{1... | collective-permute-start | bytes 688136 | tf_op jit(solution)/shard_map/ppermute | solution.py:246
  38.0 4.8 %collective-permute-start = (bf16[16,40,128]{2,1,0:T(8,128)(2,1)S(1)}, bf16[16,40,128]{2,1,0:T(8,128)(2,1)S(1)}, u32[]{:S(2)}, u32[]{:S(2)}) collective-permute-start(bf16[16,40,128]{2,1,0:T(8,128)(2,1)S(1)} %get-tuple-element.7), channel_id=1, source_target_pairs={{0,2},{2,4},{4,6},{6,8},{8,10},{10,12},{12,14},{14,30},{30,28},{28... | collective-permute-start | bytes 491528 | tf_op jit(solution)/shard_map/ppermute | solution.py:253
  38.1 6.6 %collective-permute-start.1 = (bf16[16,40,128]{2,1,0:T(8,128)(2,1)S(1)}, bf16[16,40,128]{2,1,0:T(8,128)(2,1)S(1)}, u32[]{:S(2)}, u32[]{:S(2)}) collective-permute-start(bf16[16,40,128]{2,1,0:T(8,128)(2,1)S(1)} %get-tuple-element.6), channel_id=1, source_target_pairs={{2,0},{4,2},{6,4},{8,6},{10,8},{12,10},{14,12},{30,14},{28,30},{26... | collective-permute-start | bytes 491528 | tf_op jit(solution)/shard_map/ppermute | solution.py:254

commit v2 on v1

--- a/solution.py
+++ b/solution.py
@@ -33,7 +33,7 @@
     return core, y + core * (x - y), x + core * (y - x)
 
 
-def turned(chip, count):
+def rank_of(chip, count):
     return chip % 2 * (count // 2) + chip // 2
 
 
@@ -79,9 +79,9 @@
                         edges[half] = jnp.where(lane == spot, turned, edges[half])
             start = plane * (block + rows)
             for half, values in enumerate(both(*maps)):
-                send_ref[2 * level + half, start : start + block, :] = values.astype(BF16)
+                send_ref[rank_of(2 * level + half, count), start : start + block, :] = values.astype(BF16)
         for half in range(2):
-            send_ref[2 * level + half, block : block + rows, :] = edges[half].astype(BF16)
+            send_ref[rank_of(2 * level + half, count), block : block + rows, :] = edges[half].astype(BF16)
     copies[2].wait()
     _, place, _ = places_of(lax.axis_index("gx"))
     (_, second), size = pieces(taps)
@@ -95,10 +95,12 @@
     rows = channels // count
     core, place, other = places_of(lax.axis_index("gx"))
     (_, second), size = pieces(taps)
-    filters_ref[2 * core + place] = own_ref[...]
-    filters_ref[2 * core + 1 - place] = near_ref[...]
-    filters_ref[2 - 2 * core + other] = core_ref[...]
-    filters_ref[3 - 2 * core - other] = diagonal_ref[...]
+    for chip in range(count):
+        at = rank_of(chip, count)
+        filters_ref[2 * core + place, chip] = own_ref[at]
+        filters_ref[2 * core + 1 - place, chip] = near_ref[at]
+        filters_ref[2 - 2 * core + other, chip] = core_ref[at]
+        filters_ref[3 - 2 * core - other, chip] = diagonal_ref[at]
 
     def spot(index):
         return slice(index * channels, (index + 1) * channels)
@@ -132,7 +134,8 @@
     within = lane % side
 
     def edge_of(ref, start):
-        return ref[:, start : start + rows, :].astype(F32).reshape(channels, height)
+        parts = [ref[rank_of(chip, count), start : start + rows, :] for chip in range(count)]
+        return jnp.concatenate(parts).astype(F32)
 
     own_edge, low_edge, high_edge = edge_of(own_ref, block), edge_of(low_ref, 0), edge_of(high_ref, block)
     edges = (
@@ -140,14 +143,11 @@
         own_edge,
         pltpu.roll(jnp.where(early, high_edge, own_edge), side, 1),
     )
-    planes = (
-        low_ref[:, rows : rows + block, :],
-        own_ref[:, 0:block, :],
-        own_ref[:, block + rows : 2 * block + rows, :],
-        high_ref[:, 0:block, :],
-    )
-    for at, values in enumerate(planes):
-        wide_ref[at] = values.astype(F32).reshape(channels * depth, height)
+    planes = ((low_ref, rows), (own_ref, 0), (own_ref, block + rows), (high_ref, 0))
+    for at, (ref, start) in enumerate(planes):
+        for chip in range(count):
+            values = ref[rank_of(chip, count), start : start + block, :].astype(F32)
+            wide_ref[at, chip * block : (chip + 1) * block, :] = values
 
     for c in range(3):
         for tensor in range(2):
@@ -193,7 +193,7 @@
             wide_ref[tensor, pl.ds(z, channels, stride=depth), :] = before + middle + after + extra
         for chip in range(count):
             result = wide_ref[tensor, chip * block : (chip + 1) * block, :].astype(BF16)
-            send_ref[turned(chip, count), tensor * block : (tensor + 1) * block, :] = result
+            send_ref[rank_of(chip, count), tensor * block : (tensor + 1) * block, :] = result
 
 
 def both_planes(first, second, early, side):
@@ -210,7 +210,7 @@
         pair = pair_of(level, core, count)
         for tensor, ref in enumerate((features_ref, gradient_ref)):
             start = tensor * block
-            halves = [got_ref[turned(2 * level + side, count), start : start + block, :].astype(F32) for side in range(2)]
+            halves = [got_ref[rank_of(2 * level + side, count), start : start + block, :].astype(F32) for side in range(2)]
             for plane, values in enumerate(both(*halves)):
                 ref[:, 2 * pair + plane] = values.astype(BF16).reshape(rows, depth, height)
 
@@ -237,7 +237,7 @@
         compiler_params=PARAMS,
         name="pack",
     )(*(pltpu.with_memory_space_constraint(x, pltpu.HBM) for x in (activations, out_grad, jnp.swapaxes(conv_weight, 1, 2))))
-    got = lax.all_to_all(send, CH, 0, 0, tiled=True)
+    got = lax.all_to_all(send, CH[::-1], 0, 0, tiled=True)
     own, own_filters = got[:, :span], got[:, span:]
     across_core = [(slab, slab ^ 1) for slab in range(slabs)]
     across = [(slab, slab ^ (2 if slab % 2 else 8)) for slab in range(slabs)]

time: 63.7 us -> 63.7 us (level)
    all_to_all x1, blocking collectives: 29.8 us -> 28.2 us  [local(): got = lax.all_to_all(send, CH[::-1], 0, 0, tiled=True)]
    all_to_all x1, blocking collectives: 16.1 us -> 17.7 us  [local(): back = lax.all_to_all(result, CH[::-1], 0, 0, tiled=True)]
    ppermute x1, starting transfers between devices: 0.09 us -> 1.14 us  [local(): low = lax.ppermute(got[:, block:span], ('gx', *CH), ring)]
    ppermute x1, starting transfers between devices: 1.73 us -> 0.69 us  [local(): lax.ppermute(got[:, :block + rows], ('gx', *CH), [(to, at) for at, to in...]
    ppermute x1, waiting for transfers between devices: 2.5 us -> 3.17 us  [local(): low = lax.ppermute(got[:, block:span], ('gx', *CH), ring)]
    ppermute x1, waiting for transfers between devices: 1.87 us -> 1.19 us  [local(): lax.ppermute(got[:, :block + rows], ('gx', *CH), [(to, at) for at, to in...]
where the time goes in v2:
time: 63.7 us; the launch traced here: 63.5 us
  blocking collectives  45.9 us (72%)
  waiting for transfers between devices  9.71 us (15%)
  Pallas kernels  4.52 us (7%)
  starting transfers between devices  2.6 us (4%)
  between operations  0.68 us (1%)
    all_to_all x1, blocking collectives, local(): got = lax.all_to_all(send, CH[::-1], 0, 0, tiled=True)  28.2 us
    all_to_all x1, blocking collectives, local(): back = lax.all_to_all(result, CH[::-1], 0, 0, tiled=True)  17.7 us
    ppermute x1, waiting for transfers between devices, local(): near_filters = lax.ppermute(own_filters, 'gx', across)  5.34 us
    ppermute x1, waiting for transfers between devices, local(): low = lax.ppermute(got[:, block:span], ('gx', *CH), ring)  3.17 us
    pallas_call x1, Pallas kernels, local(): pl.pallas_call(functools.partial(conv_kernel, depth=depth), out_shape=jax...  1.79 us
    pallas_call x1, Pallas kernels, local(): pl.pallas_call(pack_kernel, out_shape=jax.ShapeDtypeStruct((count, span +...  1.4 us
  transfers between devices with their start and end apart: 5, of which 3 were waited for; matrix products, arithmetic and copies ran while one was open for 0% of the time, Pallas kernels for 1%

profile of v2, /device:TPU:2, one launch (start us, length us, event | category | flops | bytes accessed | tf_op | source)
XLA Modules:
  0.0 63.5 jit_solution(9686991234811403088)
XLA Ops:
  0.6 1.4 %pack.1 = bf16[16,128,128]{2,1,0:T(8,128)(2,1)S(1)} custom-call(bf16[8,16,4,128]{3,2,1,0:T(4,128)(2,1)} %act_hbm.1, bf16[8,16,4,128]{3,2,1,0:T(4,128)(2,1)} %grad_hbm.1, bf16[27,8,128]{2,1,0:T(8,128)(2,1)} %bitcast.1), custom_call_target="tpu_custom_call" | custom-call | tf_op jit(solution)/shard_map/pack/pallas_call | solution.py:225
  2.0 28.2 %all_to_all.10 = bf16[16,128,128]{2,1,0:T(8,128)(2,1)S(1)} all-to-all(bf16[16,128,128]{2,1,0:T(8,128)(2,1)S(1)} %pack.1), channel_id=1, replica_groups=mesh['gx'=16,'level'=8,'side'=2] {'side','level'}, dimensions={0} | all-to-all | bytes 1048576 | tf_op jit(solution)/shard_map/all_to_all | solution.py:240
  30.2 0.8 %collective-permute-start.3 = (bf16[16,56,128]{2,1,0:T(8,128)(2,1)S(1)}, bf16[16,56,128]{2,1,0:T(8,128)(2,1)S(1)}, u32[]{:S(2)}, u32[]{:S(2)}) collective-permute-start(bf16[16,56,128]{2,1,0:T(8,128)(2,1)S(1)} %slice.19.own_ref), channel_id=1, source_target_pairs={{0,128},{16,48},{32,160},{48,16},{64,192},{80,112},{96,224},{112,8... | collective-permute-start | bytes 688136 | tf_op jit(solution)/shard_map/ppermute | solution.py:244
  31.0 0.0 collective-permute-start.2
  31.0 5.3 %collective-permute-done.3.near_ref = bf16[16,56,128]{2,1,0:T(8,128)(2,1)S(1)} collective-permute-done((bf16[16,56,128]{2,1,0:T(8,128)(2,1)S(1)}, bf16[16,56,128]{2,1,0:T(8,128)(2,1)S(1)}, u32[]{:S(2)}, u32[]{:S(2)}) %collective-permute-start.3) | collective-permute-done | bytes 229408 | tf_op jit(solution)/shard_map/ppermute | solution.py:244
  36.3 0.0 collective-permute-start.4
  36.4 1.1 %collective-permute-start = (bf16[16,40,128]{2,1,0:T(8,128)(2,1)S(1)}, bf16[16,40,128]{2,1,0:T(8,128)(2,1)S(1)}, u32[]{:S(2)}, u32[]{:S(2)}) collective-permute-start(bf16[16,40,128]{2,1,0:T(8,128)(2,1)S(1)} %get-tuple-element.7), channel_id=1, source_target_pairs={{0,2},{2,4},{4,6},{6,8},{8,10},{10,12},{12,14},{14,30},{30,28},{28... | collective-permute-start | bytes 491528 | tf_op jit(solution)/shard_map/ppermute | solution.py:253
  37.5 0.7 %collective-permute-start.1 = (bf16[16,40,128]{2,1,0:T(8,128)(2,1)S(1)}, bf16[16,40,128]{2,1,0:T(8,128)(2,1)S(1)}, u32[]{:S(2)}, u32[]{:S(2)}) collective-permute-start(bf16[16,40,128]{2,1,0:T(8,128)(2,1)S(1)} %get-tuple-element.6), channel_id=1, source_target_pairs={{2,0},{4,2},{6,4},{8,6},{10,8},{12,10},{14,12},{30,14},{28,30},{26... | collective-permute-start | bytes 491528 | tf_op jit(solution)/shard_map/ppermute | solution.py:254
  38.2 0.0 collective-permute-done.2.core_ref
  38.3 0.0 collective-permute-done.4.diagonal_ref
  38.3 0.4 prepare.1
  38.7 3.2 %collective-permute-done.low_ref = bf16[16,40,128]{2,1,0:T(8,128)(2,1)S(1)} collective-permute-done((bf16[16,40,128]{2,1,0:T(8,128)(2,1)S(1)}, bf16[16,40,128]{2,1,0:T(8,128)(2,1)S(1)}, u32[]{:S(2)}, u32[]{:S(2)}) %collective-permute-start) | collective-permute-done | bytes 163872 | tf_op jit(solution)/shard_map/ppermute | solution.py:253
  41.9 1.2 %collective-permute-done.1.high_ref = bf16[16,40,128]{2,1,0:T(8,128)(2,1)S(1)} collective-permute-done((bf16[16,40,128]{2,1,0:T(8,128)(2,1)S(1)}, bf16[16,40,128]{2,1,0:T(8,128)(2,1)S(1)}, u32[]{:S(2)}, u32[]{:S(2)}) %collective-permute-start.1) | collective-permute-done | bytes 163872 | tf_op jit(solution)/shard_map/ppermute | solution.py:254
  43.1 1.8 %conv.1 = bf16[16,64,128]{2,1,0:T(8,128)(2,1)S(1)} custom-call(bf16[16,72,128]{2,1,0:T(8,128)(2,1)S(1)} %slice.16.own_ref, bf16[16,40,128]{2,1,0:T(8,128)(2,1)S(1)} %collective-permute-done.low_ref, bf16[16,40,128]{2,1,0:T(8,128)(2,1)S(1)} %collective-permute-done.1.high_ref, bf16[384,1152]{1,0:T(8,128)(2,1)S(1)} %get-tuple-element.4.forward_ref, ...), custom_call_target="tpu_custom_call" | custom-call | tf_op jit(solution)/shard_map/conv/pallas_call | solution.py:265
  44.9 17.7 %all_to_all.11.got_ref = bf16[16,64,128]{2,1,0:T(8,128)(2,1)S(1)} all-to-all(bf16[16,64,128]{2,1,0:T(8,128)(2,1)S(1)} %conv.1), channel_id=1, replica_groups=mesh['gx'=16,'level'=8,'side'=2] {'side','level'}, dimensions={0} | all-to-all | bytes 524288 | tf_op jit(solution)/shard_map/all_to_all | solution.py:278
  62.6 0.9 %unpack.1 = (bf16[8,16,4,128]{3,2,1,0:T(4,128)(2,1)}, bf16[8,16,4,128]{3,2,1,0:T(4,128)(2,1)}) custom-call(bf16[16,64,128]{2,1,0:T(8,128)(2,1)S(1)} %all_to_all.11.got_ref), custom_call_target="tpu_custom_call" | custom-call | tf_op jit(solution)/shard_map/unpack/pallas_call | solution.py:279
  (3 shorter events, 0.1 us)
Async XLA Ops:
  30.2 6.1 %collective-permute-start.3 = (bf16[16,56,128]{2,1,0:T(8,128)(2,1)S(1)}, bf16[16,56,128]{2,1,0:T(8,128)(2,1)S(1)}, u32[]{:S(2)}, u32[]{:S(2)}) collective-permute-start(bf16[16,56,128]{2,1,0:T(8,128)(2,1)S(1)} %slice.19.own_ref), channel_id=1, source_target_pairs={{0,128},{16,48},{32,160},{48,16},{64,192},{80,112},{96,224},{112,8... | collective-permute-start | bytes 688136 | tf_op jit(solution)/shard_map/ppermute | solution.py:244
  31.0 7.2 %collective-permute-start.2 = (bf16[16,56,128]{2,1,0:T(8,128)(2,1)S(1)}, bf16[16,56,128]{2,1,0:T(8,128)(2,1)S(1)}, u32[]{:S(2)}, u32[]{:S(2)}) collective-permute-start(bf16[16,56,128]{2,1,0:T(8,128)(2,1)S(1)} %slice.19.own_ref), channel_id=1, source_target_pairs={{0,16},{16,0},{32,48},{48,32},{64,80},{80,64},{96,112},{112,96},{1... | collective-permute-start | bytes 688136 | tf_op jit(solution)/shard_map/ppermute | solution.py:245
  36.3 1.9 %collective-permute-start.4 = (bf16[16,56,128]{2,1,0:T(8,128)(2,1)S(1)}, bf16[16,56,128]{2,1,0:T(8,128)(2,1)S(1)}, u32[]{:S(2)}, u32[]{:S(2)}) collective-permute-start(bf16[16,56,128]{2,1,0:T(8,128)(2,1)S(1)} %collective-permute-done.3.near_ref), channel_id=1, source_target_pairs={{0,16},{16,0},{32,48},{48,32},{64,80},{80,64},{96,112},{112,96},{1... | collective-permute-start | bytes 688136 | tf_op jit(solution)/shard_map/ppermute | solution.py:246
  36.4 5.5 %collective-permute-start = (bf16[16,40,128]{2,1,0:T(8,128)(2,1)S(1)}, bf16[16,40,128]{2,1,0:T(8,128)(2,1)S(1)}, u32[]{:S(2)}, u32[]{:S(2)}) collective-permute-start(bf16[16,40,128]{2,1,0:T(8,128)(2,1)S(1)} %get-tuple-element.7), channel_id=1, source_target_pairs={{0,2},{2,4},{4,6},{6,8},{8,10},{10,12},{12,14},{14,30},{30,28},{28... | collective-permute-start | bytes 491528 | tf_op jit(solution)/shard_map/ppermute | solution.py:253
  37.5 5.6 %collective-permute-start.1 = (bf16[16,40,128]{2,1,0:T(8,128)(2,1)S(1)}, bf16[16,40,128]{2,1,0:T(8,128)(2,1)S(1)}, u32[]{:S(2)}, u32[]{:S(2)}) collective-permute-start(bf16[16,40,128]{2,1,0:T(8,128)(2,1)S(1)} %get-tuple-element.6), channel_id=1, source_target_pairs={{2,0},{4,2},{6,4},{8,6},{10,8},{12,10},{14,12},{30,14},{28,30},{26... | collective-permute-start | bytes 491528 | tf_op jit(solution)/shard_map/ppermute | solution.py:254

commit v3 on v2

--- a/solution.py
+++ b/solution.py
@@ -11,7 +11,7 @@
 VMEM = pl.BlockSpec(memory_space=pltpu.VMEM)
 HBM = pl.BlockSpec(memory_space=pltpu.HBM)
 PARAMS = pltpu.CompilerParams(vmem_limit_bytes=16 * 2**20)
-CH = ("level", "side")
+CH = ("level", "turn")
 F32 = jnp.float32
 BF16 = jnp.bfloat16
 
@@ -20,8 +20,15 @@
     return lax.broadcasted_iota(jnp.int32, shape, len(shape) - 1)
 
 
-def pair_of(level, core, count):
-    return level + core * (count // 2 - 1 - 2 * level)
+def pair_of(step, core, count):
+    return step + core * (count // 2 - 1 - 2 * step)
+
+
+def chip_of(step, side, count):
+    levels = count // 4
+    turn = step // levels
+    level = side * levels + (step if turn == 0 else 2 * levels - 1 - step)
+    return 2 * level + turn
 
 
 def pieces(taps):
@@ -61,8 +68,8 @@
     copies[0].wait()
     copies[1].wait()
     lane = lanes((rows, height))
-    for level in range(count // 2):
-        pair = pair_of(level, core, count)
+    for step in range(count // 2):
+        pair = pair_of(step, core, count)
         edges = [jnp.zeros((rows, height), F32) for _ in range(2)]
         for plane in range(2):
             maps = []
@@ -79,9 +86,9 @@
                         edges[half] = jnp.where(lane == spot, turned, edges[half])
             start = plane * (block + rows)
             for half, values in enumerate(both(*maps)):
-                send_ref[rank_of(2 * level + half, count), start : start + block, :] = values.astype(BF16)
+                send_ref[rank_of(chip_of(step, half, count), count), start : start + block, :] = values.astype(BF16)
         for half in range(2):
-            send_ref[rank_of(2 * level + half, count), block : block + rows, :] = edges[half].astype(BF16)
+            send_ref[rank_of(chip_of(step, half, count), count), block : block + rows, :] = edges[half].astype(BF16)
     copies[2].wait()
     _, place, _ = places_of(lax.axis_index("gx"))
     (_, second), size = pieces(taps)
@@ -123,7 +130,7 @@
     block = rows * depth
     channels = count * rows
     side = height // 2
-    right = lax.axis_index("side")
+    right = lax.axis_index("level") // (count // 4)
     cells_refs = (forward_cells_ref, backward_cells_ref)
 
     def spot(index):
@@ -206,11 +213,11 @@
     count, _, height = got_ref.shape
     rows, _, depth, _ = features_ref.shape
     block = rows * depth
-    for level in range(count // 2):
-        pair = pair_of(level, core, count)
+    for step in range(count // 2):
+        pair = pair_of(step, core, count)
         for tensor, ref in enumerate((features_ref, gradient_ref)):
             start = tensor * block
-            halves = [got_ref[rank_of(2 * level + side, count), start : start + block, :].astype(F32) for side in range(2)]
+            halves = [got_ref[rank_of(chip_of(step, side, count), count), start : start + block, :].astype(F32) for side in range(2)]
             for plane, values in enumerate(both(*halves)):
                 ref[:, 2 * pair + plane] = values.astype(BF16).reshape(rows, depth, height)
 
@@ -247,7 +254,9 @@
     ring = []
     for side in range(2):
         order = [
-            slab * count + 2 * pair_of(pair, slab % 2, count) + side for slab in range(slabs) for pair in range(pairs)
+            slab * count + chip_of(pair_of(pair, slab % 2, count), side, count)
+            for slab in range(slabs)
+            for pair in range(pairs)
         ]
         ring += zip(order, order[1:] + order[:1])
     low = lax.ppermute(got[:, block:span], ("gx", *CH), ring)

time: 63.7 us -> 64.2 us (level)
  no operation moved by 1% of the time
where the time goes in v3:
time: 64.2 us; the launch traced here: 63.7 us
  blocking collectives  46.1 us (72%)
  waiting for transfers between devices  9.71 us (15%)
  Pallas kernels  4.52 us (7%)
  starting transfers between devices  2.6 us (4%)
  between operations  0.68 us (1%)
    all_to_all x1, blocking collectives, local(): got = lax.all_to_all(send, CH[::-1], 0, 0, tiled=True)  28.2 us
    all_to_all x1, blocking collectives, local(): back = lax.all_to_all(result, CH[::-1], 0, 0, tiled=True)  18 us
    ppermute x1, waiting for transfers between devices, local(): near_filters = lax.ppermute(own_filters, 'gx', across)  5.34 us
    ppermute x1, waiting for transfers between devices, local(): low = lax.ppermute(got[:, block:span], ('gx', *CH), ring)  3.17 us
    pallas_call x1, Pallas kernels, local(): pl.pallas_call(functools.partial(conv_kernel, depth=depth), out_shape=jax...  1.79 us
    pallas_call x1, Pallas kernels, local(): pl.pallas_call(pack_kernel, out_shape=jax.ShapeDtypeStruct((count, span +...  1.4 us
  transfers between devices with their start and end apart: 5, of which 3 were waited for; matrix products, arithmetic and copies ran while one was open for 0% of the time, Pallas kernels for 1%

profile of v3, /device:TPU:2, one launch (start us, length us, event | category | flops | bytes accessed | tf_op | source)
XLA Modules:
  0.0 63.7 jit_solution(1829509068924156469)
XLA Ops:
  0.6 1.4 %pack.1 = bf16[16,128,128]{2,1,0:T(8,128)(2,1)S(1)} custom-call(bf16[8,16,4,128]{3,2,1,0:T(4,128)(2,1)} %act_hbm.1, bf16[8,16,4,128]{3,2,1,0:T(4,128)(2,1)} %grad_hbm.1, bf16[27,8,128]{2,1,0:T(8,128)(2,1)} %bitcast.1), custom_call_target="tpu_custom_call" | custom-call | tf_op jit(solution)/shard_map/pack/pallas_call | solution.py:232
  2.0 28.2 %all_to_all.10 = bf16[16,128,128]{2,1,0:T(8,128)(2,1)S(1)} all-to-all(bf16[16,128,128]{2,1,0:T(8,128)(2,1)S(1)} %pack.1), channel_id=1, replica_groups=mesh['gx'=16,'level'=8,'turn'=2] {'turn','level'}, dimensions={0} | all-to-all | bytes 1048576 | tf_op jit(solution)/shard_map/all_to_all | solution.py:247
  30.2 0.8 %collective-permute-start.3 = (bf16[16,56,128]{2,1,0:T(8,128)(2,1)S(1)}, bf16[16,56,128]{2,1,0:T(8,128)(2,1)S(1)}, u32[]{:S(2)}, u32[]{:S(2)}) collective-permute-start(bf16[16,56,128]{2,1,0:T(8,128)(2,1)S(1)} %slice.19.own_ref), channel_id=1, source_target_pairs={{0,128},{16,48},{32,160},{48,16},{64,192},{80,112},{96,224},{112,8... | collective-permute-start | bytes 688136 | tf_op jit(solution)/shard_map/ppermute | solution.py:251
  31.0 0.0 collective-permute-start.2
  31.0 5.3 %collective-permute-done.3.near_ref = bf16[16,56,128]{2,1,0:T(8,128)(2,1)S(1)} collective-permute-done((bf16[16,56,128]{2,1,0:T(8,128)(2,1)S(1)}, bf16[16,56,128]{2,1,0:T(8,128)(2,1)S(1)}, u32[]{:S(2)}, u32[]{:S(2)}) %collective-permute-start.3) | collective-permute-done | bytes 229408 | tf_op jit(solution)/shard_map/ppermute | solution.py:251
  36.3 0.0 collective-permute-start.4
  36.4 1.1 %collective-permute-start = (bf16[16,40,128]{2,1,0:T(8,128)(2,1)S(1)}, bf16[16,40,128]{2,1,0:T(8,128)(2,1)S(1)}, u32[]{:S(2)}, u32[]{:S(2)}) collective-permute-start(bf16[16,40,128]{2,1,0:T(8,128)(2,1)S(1)} %get-tuple-element.7), channel_id=1, source_target_pairs={{0,2},{2,4},{4,6},{6,7},{7,5},{5,3},{3,1},{1,17},{17,19},{19,21},{... | collective-permute-start | bytes 491528 | tf_op jit(solution)/shard_map/ppermute | solution.py:262
  37.5 0.7 %collective-permute-start.1 = (bf16[16,40,128]{2,1,0:T(8,128)(2,1)S(1)}, bf16[16,40,128]{2,1,0:T(8,128)(2,1)S(1)}, u32[]{:S(2)}, u32[]{:S(2)}) collective-permute-start(bf16[16,40,128]{2,1,0:T(8,128)(2,1)S(1)} %get-tuple-element.6), channel_id=1, source_target_pairs={{2,0},{4,2},{6,4},{7,6},{5,7},{3,5},{1,3},{17,1},{19,17},{21,19},{... | collective-permute-start | bytes 491528 | tf_op jit(solution)/shard_map/ppermute | solution.py:263
  38.2 0.0 collective-permute-done.2.core_ref
  38.3 0.0 collective-permute-done.4.diagonal_ref
  38.3 0.4 prepare.1
  38.7 3.2 %collective-permute-done.low_ref = bf16[16,40,128]{2,1,0:T(8,128)(2,1)S(1)} collective-permute-done((bf16[16,40,128]{2,1,0:T(8,128)(2,1)S(1)}, bf16[16,40,128]{2,1,0:T(8,128)(2,1)S(1)}, u32[]{:S(2)}, u32[]{:S(2)}) %collective-permute-start) | collective-permute-done | bytes 163872 | tf_op jit(solution)/shard_map/ppermute | solution.py:262
  41.9 1.2 %collective-permute-done.1.high_ref = bf16[16,40,128]{2,1,0:T(8,128)(2,1)S(1)} collective-permute-done((bf16[16,40,128]{2,1,0:T(8,128)(2,1)S(1)}, bf16[16,40,128]{2,1,0:T(8,128)(2,1)S(1)}, u32[]{:S(2)}, u32[]{:S(2)}) %collective-permute-start.1) | collective-permute-done | bytes 163872 | tf_op jit(solution)/shard_map/ppermute | solution.py:263
  43.1 1.8 %conv.1 = bf16[16,64,128]{2,1,0:T(8,128)(2,1)S(1)} custom-call(bf16[16,72,128]{2,1,0:T(8,128)(2,1)S(1)} %slice.16.own_ref, bf16[16,40,128]{2,1,0:T(8,128)(2,1)S(1)} %collective-permute-done.low_ref, bf16[16,40,128]{2,1,0:T(8,128)(2,1)S(1)} %collective-permute-done.1.high_ref, bf16[384,1152]{1,0:T(8,128)(2,1)S(1)} %get-tuple-element.4.forward_ref, ...), custom_call_target="tpu_custom_call" | custom-call | tf_op jit(solution)/shard_map/conv/pallas_call | solution.py:274
  44.9 18.0 %all_to_all.11.got_ref = bf16[16,64,128]{2,1,0:T(8,128)(2,1)S(1)} all-to-all(bf16[16,64,128]{2,1,0:T(8,128)(2,1)S(1)} %conv.1), channel_id=1, replica_groups=mesh['gx'=16,'level'=8,'turn'=2] {'turn','level'}, dimensions={0} | all-to-all | bytes 524288 | tf_op jit(solution)/shard_map/all_to_all | solution.py:287
  62.8 0.9 %unpack.1 = (bf16[8,16,4,128]{3,2,1,0:T(4,128)(2,1)}, bf16[8,16,4,128]{3,2,1,0:T(4,128)(2,1)}) custom-call(bf16[16,64,128]{2,1,0:T(8,128)(2,1)S(1)} %all_to_all.11.got_ref), custom_call_target="tpu_custom_call" | custom-call | tf_op jit(solution)/shard_map/unpack/pallas_call | solution.py:288
  (3 shorter events, 0.1 us)
Async XLA Ops:
  30.2 6.1 %collective-permute-start.3 = (bf16[16,56,128]{2,1,0:T(8,128)(2,1)S(1)}, bf16[16,56,128]{2,1,0:T(8,128)(2,1)S(1)}, u32[]{:S(2)}, u32[]{:S(2)}) collective-permute-start(bf16[16,56,128]{2,1,0:T(8,128)(2,1)S(1)} %slice.19.own_ref), channel_id=1, source_target_pairs={{0,128},{16,48},{32,160},{48,16},{64,192},{80,112},{96,224},{112,8... | collective-permute-start | bytes 688136 | tf_op jit(solution)/shard_map/ppermute | solution.py:251
  31.0 7.2 %collective-permute-start.2 = (bf16[16,56,128]{2,1,0:T(8,128)(2,1)S(1)}, bf16[16,56,128]{2,1,0:T(8,128)(2,1)S(1)}, u32[]{:S(2)}, u32[]{:S(2)}) collective-permute-start(bf16[16,56,128]{2,1,0:T(8,128)(2,1)S(1)} %slice.19.own_ref), channel_id=1, source_target_pairs={{0,16},{16,0},{32,48},{48,32},{64,80},{80,64},{96,112},{112,96},{1... | collective-permute-start | bytes 688136 | tf_op jit(solution)/shard_map/ppermute | solution.py:252
  36.3 1.9 %collective-permute-start.4 = (bf16[16,56,128]{2,1,0:T(8,128)(2,1)S(1)}, bf16[16,56,128]{2,1,0:T(8,128)(2,1)S(1)}, u32[]{:S(2)}, u32[]{:S(2)}) collective-permute-start(bf16[16,56,128]{2,1,0:T(8,128)(2,1)S(1)} %collective-permute-done.3.near_ref), channel_id=1, source_target_pairs={{0,16},{16,0},{32,48},{48,32},{64,80},{80,64},{96,112},{112,96},{1... | collective-permute-start | bytes 688136 | tf_op jit(solution)/shard_map/ppermute | solution.py:253
  36.4 5.5 %collective-permute-start = (bf16[16,40,128]{2,1,0:T(8,128)(2,1)S(1)}, bf16[16,40,128]{2,1,0:T(8,128)(2,1)S(1)}, u32[]{:S(2)}, u32[]{:S(2)}) collective-permute-start(bf16[16,40,128]{2,1,0:T(8,128)(2,1)S(1)} %get-tuple-element.7), channel_id=1, source_target_pairs={{0,2},{2,4},{4,6},{6,7},{7,5},{5,3},{3,1},{1,17},{17,19},{19,21},{... | collective-permute-start | bytes 491528 | tf_op jit(solution)/shard_map/ppermute | solution.py:262
  37.5 5.6 %collective-permute-start.1 = (bf16[16,40,128]{2,1,0:T(8,128)(2,1)S(1)}, bf16[16,40,128]{2,1,0:T(8,128)(2,1)S(1)}, u32[]{:S(2)}, u32[]{:S(2)}) collective-permute-start(bf16[16,40,128]{2,1,0:T(8,128)(2,1)S(1)} %get-tuple-element.6), channel_id=1, source_target_pairs={{2,0},{4,2},{6,4},{7,6},{5,7},{3,5},{1,3},{17,1},{19,17},{21,19},{... | collective-permute-start | bytes 491528 | tf_op jit(solution)/shard_map/ppermute | solution.py:263

commit v4 on v2

--- a/solution.py
+++ b/solution.py
@@ -31,6 +31,10 @@
 def places_of(slab):
     core, x, y = lax.rem(slab, 2), lax.rem(slab // 2, 2), slab // 8
     return core, y + core * (x - y), x + core * (y - x)
+
+
+def odd(slab, level):
+    return lax.rem(slab + level, 2)
 
 
 def rank_of(chip, count):
@@ -116,7 +120,7 @@
                 backward_ref[spot(b), spot(3 * c + a)] = matrix.T
 
 
-def conv_kernel(own_ref, low_ref, high_ref, forward_ref, backward_ref, send_ref,
+def conv_kernel(own_ref, outer_ref, inner_ref, forward_ref, backward_ref, send_ref,
                 forward_cells_ref, backward_cells_ref, wide_ref, *, depth):
     count, span, height = own_ref.shape
     rows = span // (2 * depth + 1)
@@ -133,21 +137,38 @@
     early = lane < side
     within = lane % side
 
-    def edge_of(ref, start):
-        parts = [ref[rank_of(chip, count), start : start + rows, :] for chip in range(count)]
-        return jnp.concatenate(parts).astype(F32)
-
-    own_edge, low_edge, high_edge = edge_of(own_ref, block), edge_of(low_ref, 0), edge_of(high_ref, block)
+    is_odd = odd(lax.axis_index("gx"), lax.axis_index("level")) == 1
+
+    def own_part(start, size):
+        return lambda at: own_ref[at, start : start + size, :].astype(F32)
+
+    def halo_part(first_ref, second_ref, start, size):
+        def part(at):
+            first, second = (ref[at, start : start + size, :].astype(F32) for ref in (first_ref, second_ref))
+            return jnp.where(is_odd, first, second)
+
+        return part
+
+    def edge_of(part):
+        return jnp.concatenate([part(rank_of(chip, count)) for chip in range(count)])
+
+    own_edge = edge_of(own_part(block, rows))
+    low_edge = edge_of(halo_part(inner_ref, outer_ref, 0, rows))
+    high_edge = edge_of(halo_part(outer_ref, inner_ref, block, rows))
     edges = (
         pltpu.roll(jnp.where(early, own_edge, low_edge), side, 1),
         own_edge,
         pltpu.roll(jnp.where(early, high_edge, own_edge), side, 1),
     )
-    planes = ((low_ref, rows), (own_ref, 0), (own_ref, block + rows), (high_ref, 0))
-    for at, (ref, start) in enumerate(planes):
+    planes = (
+        halo_part(inner_ref, outer_ref, rows, block),
+        own_part(0, block),
+        own_part(block + rows, block),
+        halo_part(outer_ref, inner_ref, 0, block),
+    )
+    for at, part in enumerate(planes):
         for chip in range(count):
-            values = ref[rank_of(chip, count), start : start + block, :].astype(F32)
-            wide_ref[at, chip * block : (chip + 1) * block, :] = values
+            wide_ref[at, chip * block : (chip + 1) * block, :] = part(rank_of(chip, count))
 
     for c in range(3):
         for tensor in range(2):
@@ -244,14 +265,18 @@
     near_filters = lax.ppermute(own_filters, "gx", across)
     core_filters = lax.ppermute(own_filters, "gx", across_core)
     diagonal_filters = lax.ppermute(near_filters, "gx", across_core)
-    ring = []
+    swaps = [], []
     for side in range(2):
-        order = [
+        chain = [
             slab * count + 2 * pair_of(pair, slab % 2, count) + side for slab in range(slabs) for pair in range(pairs)
         ]
-        ring += zip(order, order[1:] + order[:1])
-    low = lax.ppermute(got[:, block:span], ("gx", *CH), ring)
-    high = lax.ppermute(got[:, : block + rows], ("gx", *CH), [(to, at) for at, to in ring])
+        for at, device in enumerate(chain):
+            after = chain[(at + 1) % len(chain)]
+            swaps[at % 2].extend(((device, after), (after, device)))
+    is_odd = odd(lax.axis_index("gx"), lax.axis_index("level")) == 1
+    lower, upper = got[:, : block + rows], got[:, block:span]
+    outer = lax.ppermute(jnp.where(is_odd, upper, lower), ("gx", *CH), swaps[1])
+    inner = lax.ppermute(jnp.where(is_odd, lower, upper), ("gx", *CH), swaps[0])
     forward, backward = pl.pallas_call(
         functools.partial(prepare_kernel, taps=taps),
         out_shape=[jax.ShapeDtypeStruct((3 * channels, 9 * channels), BF16)] * 2,
@@ -274,7 +299,7 @@
         ],
         compiler_params=PARAMS,
         name="conv",
-    )(own, low, high, forward, backward)
+    )(own, outer, inner, forward, backward)
     back = lax.all_to_all(result, CH[::-1], 0, 0, tiled=True)
     return pl.pallas_call(
         unpack_kernel,

time: 63.7 us -> 63.7 us (level)
  transfers between devices with their start and end apart: 5 -> 5, of which waited for: 3 -> 2; matrix products, arithmetic and copies ran while one was open for 0% -> 0% of each run, Pallas kernels for 1% -> 1%
where the time goes in v4:
time: 63.7 us; the launch traced here: 63.2 us
  blocking collectives  45.6 us (72%)
  waiting for transfers between devices  10 us (16%)
  Pallas kernels  4.53 us (7%)
  starting transfers between devices  2.29 us (4%)
  between operations  0.68 us (1%)
    all_to_all x1, blocking collectives, local(): got = lax.all_to_all(send, CH[::-1], 0, 0, tiled=True)  28.2 us
    all_to_all x1, blocking collectives, local(): back = lax.all_to_all(result, CH[::-1], 0, 0, tiled=True)  17.5 us
    ppermute x1, waiting for transfers between devices, local(): near_filters = lax.ppermute(own_filters, 'gx', across)  5.34 us
    ppermute x1, waiting for transfers between devices, local(): inner = lax.ppermute(jnp.where(is_odd, lower, upper), ('gx', *CH), swaps[0])  4.68 us
    pallas_call x1, Pallas kernels, local(): pl.pallas_call(functools.partial(conv_kernel, depth=depth), out_shape=jax...  1.8 us
    pallas_call x1, Pallas kernels, local(): pl.pallas_call(pack_kernel, out_shape=jax.ShapeDtypeStruct((count, span +...  1.4 us
  transfers between devices with their start and end apart: 5, of which 2 were waited for; matrix products, arithmetic and copies ran while one was open for 0% of the time, Pallas kernels for 1%

profile of v4, /device:TPU:2, one launch (start us, length us, event | category | flops | bytes accessed | tf_op | source)
XLA Modules:
  0.0 63.2 jit_solution(460286792773717869)
XLA Ops:
  0.6 1.4 %pack.1 = bf16[16,128,128]{2,1,0:T(8,128)(2,1)S(1)} custom-call(bf16[8,16,4,128]{3,2,1,0:T(4,128)(2,1)} %act_hbm.1, bf16[8,16,4,128]{3,2,1,0:T(4,128)(2,1)} %grad_hbm.1, bf16[27,8,128]{2,1,0:T(8,128)(2,1)} %bitcast.1), custom_call_target="tpu_custom_call" | custom-call | tf_op jit(solution)/shard_map/pack/pallas_call | solution.py:246
  2.0 28.2 %all_to_all.10 = bf16[16,128,128]{2,1,0:T(8,128)(2,1)S(1)} all-to-all(bf16[16,128,128]{2,1,0:T(8,128)(2,1)S(1)} %pack.1), channel_id=1, replica_groups=mesh['gx'=16,'level'=8,'side'=2] {'side','level'}, dimensions={0} | all-to-all | bytes 1048576 | tf_op jit(solution)/shard_map/all_to_all | solution.py:261
  30.2 0.8 %collective-permute-start.3 = (bf16[16,56,128]{2,1,0:T(8,128)(2,1)S(1)}, bf16[16,56,128]{2,1,0:T(8,128)(2,1)S(1)}, u32[]{:S(2)}, u32[]{:S(2)}) collective-permute-start(bf16[16,56,128]{2,1,0:T(8,128)(2,1)S(1)} %slice.19.own_ref), channel_id=1, source_target_pairs={{0,128},{16,48},{32,160},{48,16},{64,192},{80,112},{96,224},{112,8... | collective-permute-start | bytes 688136 | tf_op jit(solution)/shard_map/ppermute | solution.py:265
  31.0 0.0 collective-permute-start.2
  31.0 5.3 %collective-permute-done.3.near_ref = bf16[16,56,128]{2,1,0:T(8,128)(2,1)S(1)} collective-permute-done((bf16[16,56,128]{2,1,0:T(8,128)(2,1)S(1)}, bf16[16,56,128]{2,1,0:T(8,128)(2,1)S(1)}, u32[]{:S(2)}, u32[]{:S(2)}) %collective-permute-start.3) | collective-permute-done | bytes 229408 | tf_op jit(solution)/shard_map/ppermute | solution.py:265
  36.3 0.0 collective-permute-start.4
  36.4 1.2 %collective-permute-start.1 = (bf16[16,40,128]{2,1,0:T(8,128)(2,1)S(1)}, bf16[16,40,128]{2,1,0:T(8,128)(2,1)S(1)}, u32[]{:S(2)}, u32[]{:S(2)}) collective-permute-start(bf16[16,40,128]{2,1,0:T(8,128)(2,1)S(1)} %get-tuple-element.6), channel_id=1, source_target_pairs={{0,2},{2,0},{4,6},{6,4},{8,10},{10,8},{12,14},{14,12},{30,28},{28,... | collective-permute-start | bytes 491528 | tf_op jit(solution)/shard_map/ppermute | solution.py:279
  37.5 0.4 collective-permute-start
  37.9 0.0 collective-permute-done.2.core_ref
  37.9 0.0 collective-permute-done.4.diagonal_ref
  37.9 0.4 prepare.1
  38.4 4.7 %collective-permute-done.1.inner_ref = bf16[16,40,128]{2,1,0:T(8,128)(2,1)S(1)} collective-permute-done((bf16[16,40,128]{2,1,0:T(8,128)(2,1)S(1)}, bf16[16,40,128]{2,1,0:T(8,128)(2,1)S(1)}, u32[]{:S(2)}, u32[]{:S(2)}) %collective-permute-start.1) | collective-permute-done | bytes 163872 | tf_op jit(solution)/shard_map/ppermute | solution.py:279
  43.1 0.0 collective-permute-done.outer_ref
  43.1 1.8 %conv.1 = bf16[16,64,128]{2,1,0:T(8,128)(2,1)S(1)} custom-call(bf16[16,72,128]{2,1,0:T(8,128)(2,1)S(1)} %slice.16.own_ref, bf16[16,40,128]{2,1,0:T(8,128)(2,1)S(1)} %collective-permute-done.outer_ref, bf16[16,40,128]{2,1,0:T(8,128)(2,1)S(1)} %collective-permute-done.1.inner_ref, bf16[384,1152]{1,0:T(8,128)(2,1)S(1)} %get-tuple-element.4.forward_ref, ...), custom_call_target="tpu_custom_call" | custom-call | tf_op jit(solution)/shard_map/conv/pallas_call | solution.py:290
  44.9 17.5 %all_to_all.11.got_ref = bf16[16,64,128]{2,1,0:T(8,128)(2,1)S(1)} all-to-all(bf16[16,64,128]{2,1,0:T(8,128)(2,1)S(1)} %conv.1), channel_id=1, replica_groups=mesh['gx'=16,'level'=8,'side'=2] {'side','level'}, dimensions={0} | all-to-all | bytes 524288 | tf_op jit(solution)/shard_map/all_to_all | solution.py:303
  62.3 0.9 %unpack.1 = (bf16[8,16,4,128]{3,2,1,0:T(4,128)(2,1)}, bf16[8,16,4,128]{3,2,1,0:T(4,128)(2,1)}) custom-call(bf16[16,64,128]{2,1,0:T(8,128)(2,1)S(1)} %all_to_all.11.got_ref), custom_call_target="tpu_custom_call" | custom-call | tf_op jit(solution)/shard_map/unpack/pallas_call | solution.py:304
  (3 shorter events, 0.1 us)
Async XLA Ops:
  30.2 6.1 %collective-permute-start.3 = (bf16[16,56,128]{2,1,0:T(8,128)(2,1)S(1)}, bf16[16,56,128]{2,1,0:T(8,128)(2,1)S(1)}, u32[]{:S(2)}, u32[]{:S(2)}) collective-permute-start(bf16[16,56,128]{2,1,0:T(8,128)(2,1)S(1)} %slice.19.own_ref), channel_id=1, source_target_pairs={{0,128},{16,48},{32,160},{48,16},{64,192},{80,112},{96,224},{112,8... | collective-permute-start | bytes 688136 | tf_op jit(solution)/shard_map/ppermute | solution.py:265
  31.0 6.9 %collective-permute-start.2 = (bf16[16,56,128]{2,1,0:T(8,128)(2,1)S(1)}, bf16[16,56,128]{2,1,0:T(8,128)(2,1)S(1)}, u32[]{:S(2)}, u32[]{:S(2)}) collective-permute-start(bf16[16,56,128]{2,1,0:T(8,128)(2,1)S(1)} %slice.19.own_ref), channel_id=1, source_target_pairs={{0,16},{16,0},{32,48},{48,32},{64,80},{80,64},{96,112},{112,96},{1... | collective-permute-start | bytes 688136 | tf_op jit(solution)/shard_map/ppermute | solution.py:266
  36.3 1.6 %collective-permute-start.4 = (bf16[16,56,128]{2,1,0:T(8,128)(2,1)S(1)}, bf16[16,56,128]{2,1,0:T(8,128)(2,1)S(1)}, u32[]{:S(2)}, u32[]{:S(2)}) collective-permute-start(bf16[16,56,128]{2,1,0:T(8,128)(2,1)S(1)} %collective-permute-done.3.near_ref), channel_id=1, source_target_pairs={{0,16},{16,0},{32,48},{48,32},{64,80},{80,64},{96,112},{112,96},{1... | collective-permute-start | bytes 688136 | tf_op jit(solution)/shard_map/ppermute | solution.py:267
  36.4 6.7 %collective-permute-start.1 = (bf16[16,40,128]{2,1,0:T(8,128)(2,1)S(1)}, bf16[16,40,128]{2,1,0:T(8,128)(2,1)S(1)}, u32[]{:S(2)}, u32[]{:S(2)}) collective-permute-start(bf16[16,40,128]{2,1,0:T(8,128)(2,1)S(1)} %get-tuple-element.6), channel_id=1, source_target_pairs={{0,2},{2,0},{4,6},{6,4},{8,10},{10,8},{12,14},{14,12},{30,28},{28,... | collective-permute-start | bytes 491528 | tf_op jit(solution)/shard_map/ppermute | solution.py:279
  37.5 5.5 %collective-permute-start = (bf16[16,40,128]{2,1,0:T(8,128)(2,1)S(1)}, bf16[16,40,128]{2,1,0:T(8,128)(2,1)S(1)}, u32[]{:S(2)}, u32[]{:S(2)}) collective-permute-start(bf16[16,40,128]{2,1,0:T(8,128)(2,1)S(1)} %get-tuple-element.7), channel_id=1, source_target_pairs={{2,4},{4,2},{6,8},{8,6},{10,12},{12,10},{14,30},{30,14},{28,26},{2... | collective-permute-start | bytes 491528 | tf_op jit(solution)/shard_map/ppermute | solution.py:278

commit v5 on v2

--- a/solution.py
+++ b/solution.py
@@ -31,6 +31,10 @@
 def places_of(slab):
     core, x, y = lax.rem(slab, 2), lax.rem(slab // 2, 2), slab // 8
     return core, y + core * (x - y), x + core * (y - x)
+
+
+def odd(slab, level):
+    return lax.rem(slab + level, 2)
 
 
 def rank_of(chip, count):
@@ -77,9 +81,10 @@
                         edge = side - half
                         turned = pltpu.roll(column, (spot - edge) % height, 1)
                         edges[half] = jnp.where(lane == spot, turned, edges[half])
-            start = plane * (block + rows)
+            place = plane + lax.rem(pair, 2) * (1 - 2 * plane)
+            start = pl.multiple_of(place * (block + rows), 8)
             for half, values in enumerate(both(*maps)):
-                send_ref[rank_of(2 * level + half, count), start : start + block, :] = values.astype(BF16)
+                send_ref[rank_of(2 * level + half, count), pl.ds(start, block), :] = values.astype(BF16)
         for half in range(2):
             send_ref[rank_of(2 * level + half, count), block : block + rows, :] = edges[half].astype(BF16)
     copies[2].wait()
@@ -116,7 +121,7 @@
                 backward_ref[spot(b), spot(3 * c + a)] = matrix.T
 
 
-def conv_kernel(own_ref, low_ref, high_ref, forward_ref, backward_ref, send_ref,
+def conv_kernel(own_ref, outer_ref, inner_ref, forward_ref, backward_ref, send_ref,
                 forward_cells_ref, backward_cells_ref, wide_ref, *, depth):
     count, span, height = own_ref.shape
     rows = span // (2 * depth + 1)
@@ -133,18 +138,27 @@
     early = lane < side
     within = lane % side
 
+    is_odd = odd(lax.axis_index("gx"), lax.axis_index("level"))
+
     def edge_of(ref, start):
         parts = [ref[rank_of(chip, count), start : start + rows, :] for chip in range(count)]
         return jnp.concatenate(parts).astype(F32)
 
-    own_edge, low_edge, high_edge = edge_of(own_ref, block), edge_of(low_ref, 0), edge_of(high_ref, block)
+    own_edge, outer_edge, inner_edge = edge_of(own_ref, block), edge_of(outer_ref, block), edge_of(inner_ref, 0)
+    low_edge = jnp.where(is_odd == 1, inner_edge, outer_edge)
+    high_edge = jnp.where(is_odd == 1, outer_edge, inner_edge)
     edges = (
         pltpu.roll(jnp.where(early, own_edge, low_edge), side, 1),
         own_edge,
         pltpu.roll(jnp.where(early, high_edge, own_edge), side, 1),
     )
-    planes = ((low_ref, rows), (own_ref, 0), (own_ref, block + rows), (high_ref, 0))
-    for at, (ref, start) in enumerate(planes):
+    planes = (
+        (3 * is_odd, outer_ref, 0),
+        (1 + is_odd, own_ref, 0),
+        (2 - is_odd, own_ref, block + rows),
+        (3 - 3 * is_odd, inner_ref, rows),
+    )
+    for at, ref, start in planes:
         for chip in range(count):
             values = ref[rank_of(chip, count), start : start + block, :].astype(F32)
             wide_ref[at, chip * block : (chip + 1) * block, :] = values
@@ -244,14 +258,16 @@
     near_filters = lax.ppermute(own_filters, "gx", across)
     core_filters = lax.ppermute(own_filters, "gx", across_core)
     diagonal_filters = lax.ppermute(near_filters, "gx", across_core)
-    ring = []
+    swaps = [], []
     for side in range(2):
-        order = [
+        chain = [
             slab * count + 2 * pair_of(pair, slab % 2, count) + side for slab in range(slabs) for pair in range(pairs)
         ]
-        ring += zip(order, order[1:] + order[:1])
-    low = lax.ppermute(got[:, block:span], ("gx", *CH), ring)
-    high = lax.ppermute(got[:, : block + rows], ("gx", *CH), [(to, at) for at, to in ring])
+        for at, device in enumerate(chain):
+            after = chain[(at + 1) % len(chain)]
+            swaps[at % 2].extend(((device, after), (after, device)))
+    outer = lax.ppermute(got[:, : block + rows], ("gx", *CH), swaps[1])
+    inner = lax.ppermute(got[:, block:span], ("gx", *CH), swaps[0])
     forward, backward = pl.pallas_call(
         functools.partial(prepare_kernel, taps=taps),
         out_shape=[jax.ShapeDtypeStruct((3 * channels, 9 * channels), BF16)] * 2,
@@ -274,7 +290,7 @@
         ],
         compiler_params=PARAMS,
         name="conv",
-    )(own, low, high, forward, backward)
+    )(own, outer, inner, forward, backward)
     back = lax.all_to_all(result, CH[::-1], 0, 0, tiled=True)
     return pl.pallas_call(
         unpack_kernel,

time: 63.7 us -> 64 us (level)
  waiting for transfers between devices: 9.71 us -> 11.4 us
  blocking collectives: 45.9 us -> 44.9 us
    ppermute x2, waiting for transfers between devices: 4.37 us -> 5.9 us  [the longest x1 2.97 us: local(): inner = lax.ppermute(got[:, block:span], ('gx', *CH), swaps[0])]
    all_to_all x1, blocking collectives: 17.7 us -> 16.7 us  [local(): back = lax.all_to_all(result, CH[::-1], 0, 0, tiled=True)]
  transfers between devices with their start and end apart: 5 -> 5, of which waited for: 3 -> 4; matrix products, arithmetic and copies ran while one was open for 0% -> 0% of each run, Pallas kernels for 1% -> 1%
where the time goes in v5:
time: 64 us; the launch traced here: 63.6 us
  blocking collectives  44.9 us (70%)
  waiting for transfers between devices  11.4 us (18%)
  Pallas kernels  4.54 us (7%)
  starting transfers between devices  2.02 us (3%)
  between operations  0.67 us (1%)
    all_to_all x1, blocking collectives, local(): got = lax.all_to_all(send, CH[::-1], 0, 0, tiled=True)  28.2 us
    all_to_all x1, blocking collectives, local(): back = lax.all_to_all(result, CH[::-1], 0, 0, tiled=True)  16.7 us
    ppermute x1, waiting for transfers between devices, local(): near_filters = lax.ppermute(own_filters, 'gx', across)  5.34 us
    ppermute x1, waiting for transfers between devices, local(): inner = lax.ppermute(got[:, block:span], ('gx', *CH), swaps[0])  2.97 us
    ppermute x1, waiting for transfers between devices, local(): outer = lax.ppermute(got[:, :block + rows], ('gx', *CH), swaps[1])  2.93 us
    pallas_call x1, Pallas kernels, local(): pl.pallas_call(functools.partial(conv_kernel, depth=depth), out_shape=jax...  1.82 us
    pallas_call x1, Pallas kernels, local(): pl.pallas_call(pack_kernel, out_shape=jax.ShapeDtypeStruct((count, span +...  1.4 us
  transfers between devices with their start and end apart: 5, of which 4 were waited for; matrix products, arithmetic and copies ran while one was open for 0% of the time, Pallas kernels for 1%

profile of v5, /device:TPU:2, one launch (start us, length us, event | category | flops | bytes accessed | tf_op | source)
XLA Modules:
  0.0 63.6 jit_solution(5773630382586716586)
XLA Ops:
  0.6 1.4 %pack.1 = bf16[16,128,128]{2,1,0:T(8,128)(2,1)S(1)} custom-call(bf16[8,16,4,128]{3,2,1,0:T(4,128)(2,1)} %act_hbm.1, bf16[8,16,4,128]{3,2,1,0:T(4,128)(2,1)} %grad_hbm.1, bf16[27,8,128]{2,1,0:T(8,128)(2,1)} %bitcast.1), custom_call_target="tpu_custom_call" | custom-call | tf_op jit(solution)/shard_map/pack/pallas_call | solution.py:239
  2.0 28.2 %all_to_all.10 = bf16[16,128,128]{2,1,0:T(8,128)(2,1)S(1)} all-to-all(bf16[16,128,128]{2,1,0:T(8,128)(2,1)S(1)} %pack.1), channel_id=1, replica_groups=mesh['gx'=16,'level'=8,'side'=2] {'side','level'}, dimensions={0} | all-to-all | bytes 1048576 | tf_op jit(solution)/shard_map/all_to_all | solution.py:254
  30.2 0.8 %collective-permute-start.3 = (bf16[16,56,128]{2,1,0:T(8,128)(2,1)S(1)}, bf16[16,56,128]{2,1,0:T(8,128)(2,1)S(1)}, u32[]{:S(2)}, u32[]{:S(2)}) collective-permute-start(bf16[16,56,128]{2,1,0:T(8,128)(2,1)S(1)} %slice.19.own_ref), channel_id=1, source_target_pairs={{0,128},{16,48},{32,160},{48,16},{64,192},{80,112},{96,224},{112,8... | collective-permute-start | bytes 688136 | tf_op jit(solution)/shard_map/ppermute | solution.py:258
  31.0 0.0 collective-permute-start.2
  31.0 5.3 %collective-permute-done.3.near_ref = bf16[16,56,128]{2,1,0:T(8,128)(2,1)S(1)} collective-permute-done((bf16[16,56,128]{2,1,0:T(8,128)(2,1)S(1)}, bf16[16,56,128]{2,1,0:T(8,128)(2,1)S(1)}, u32[]{:S(2)}, u32[]{:S(2)}) %collective-permute-start.3) | collective-permute-done | bytes 229408 | tf_op jit(solution)/shard_map/ppermute | solution.py:258
  36.3 0.0 collective-permute-start.4
  36.4 0.7 %collective-permute-start = (bf16[16,40,128]{2,1,0:T(8,128)(2,1)S(1)}, bf16[16,40,128]{2,1,0:T(8,128)(2,1)S(1)}, u32[]{:S(2)}, u32[]{:S(2)}) collective-permute-start(bf16[16,40,128]{2,1,0:T(8,128)(2,1)S(1)} %get-tuple-element.7), channel_id=1, source_target_pairs={{2,4},{4,2},{6,8},{8,6},{10,12},{12,10},{14,30},{30,14},{28,26},{2... | collective-permute-start | bytes 491528 | tf_op jit(solution)/shard_map/ppermute | solution.py:269
  37.1 0.5 collective-permute-start.1
  37.7 0.0 collective-permute-done.2.core_ref
  37.7 0.2 collective-permute-done.4.diagonal_ref
  37.8 0.4 prepare.1
  38.3 2.9 %collective-permute-done.outer_ref = bf16[16,40,128]{2,1,0:T(8,128)(2,1)S(1)} collective-permute-done((bf16[16,40,128]{2,1,0:T(8,128)(2,1)S(1)}, bf16[16,40,128]{2,1,0:T(8,128)(2,1)S(1)}, u32[]{:S(2)}, u32[]{:S(2)}) %collective-permute-start) | collective-permute-done | bytes 163872 | tf_op jit(solution)/shard_map/ppermute | solution.py:269
  41.2 3.0 %collective-permute-done.1.inner_ref = bf16[16,40,128]{2,1,0:T(8,128)(2,1)S(1)} collective-permute-done((bf16[16,40,128]{2,1,0:T(8,128)(2,1)S(1)}, bf16[16,40,128]{2,1,0:T(8,128)(2,1)S(1)}, u32[]{:S(2)}, u32[]{:S(2)}) %collective-permute-start.1) | collective-permute-done | bytes 163872 | tf_op jit(solution)/shard_map/ppermute | solution.py:270
  44.2 1.8 %conv.1 = bf16[16,64,128]{2,1,0:T(8,128)(2,1)S(1)} custom-call(bf16[16,72,128]{2,1,0:T(8,128)(2,1)S(1)} %slice.16.own_ref, bf16[16,40,128]{2,1,0:T(8,128)(2,1)S(1)} %collective-permute-done.outer_ref, bf16[16,40,128]{2,1,0:T(8,128)(2,1)S(1)} %collective-permute-done.1.inner_ref, bf16[384,1152]{1,0:T(8,128)(2,1)S(1)} %get-tuple-element.4.forward_ref, ...), custom_call_target="tpu_custom_call" | custom-call | tf_op jit(solution)/shard_map/conv/pallas_call | solution.py:281
  46.0 16.7 %all_to_all.11.got_ref = bf16[16,64,128]{2,1,0:T(8,128)(2,1)S(1)} all-to-all(bf16[16,64,128]{2,1,0:T(8,128)(2,1)S(1)} %conv.1), channel_id=1, replica_groups=mesh['gx'=16,'level'=8,'side'=2] {'side','level'}, dimensions={0} | all-to-all | bytes 524288 | tf_op jit(solution)/shard_map/all_to_all | solution.py:294
  62.7 0.9 %unpack.1 = (bf16[8,16,4,128]{3,2,1,0:T(4,128)(2,1)}, bf16[8,16,4,128]{3,2,1,0:T(4,128)(2,1)}) custom-call(bf16[16,64,128]{2,1,0:T(8,128)(2,1)S(1)} %all_to_all.11.got_ref), custom_call_target="tpu_custom_call" | custom-call | tf_op jit(solution)/shard_map/unpack/pallas_call | solution.py:295
  (3 shorter events, 0.1 us)
Async XLA Ops:
  30.2 6.1 %collective-permute-start.3 = (bf16[16,56,128]{2,1,0:T(8,128)(2,1)S(1)}, bf16[16,56,128]{2,1,0:T(8,128)(2,1)S(1)}, u32[]{:S(2)}, u32[]{:S(2)}) collective-permute-start(bf16[16,56,128]{2,1,0:T(8,128)(2,1)S(1)} %slice.19.own_ref), channel_id=1, source_target_pairs={{0,128},{16,48},{32,160},{48,16},{64,192},{80,112},{96,224},{112,8... | collective-permute-start | bytes 688136 | tf_op jit(solution)/shard_map/ppermute | solution.py:258
  31.0 6.7 %collective-permute-start.2 = (bf16[16,56,128]{2,1,0:T(8,128)(2,1)S(1)}, bf16[16,56,128]{2,1,0:T(8,128)(2,1)S(1)}, u32[]{:S(2)}, u32[]{:S(2)}) collective-permute-start(bf16[16,56,128]{2,1,0:T(8,128)(2,1)S(1)} %slice.19.own_ref), channel_id=1, source_target_pairs={{0,16},{16,0},{32,48},{48,32},{64,80},{80,64},{96,112},{112,96},{1... | collective-permute-start | bytes 688136 | tf_op jit(solution)/shard_map/ppermute | solution.py:259
  36.3 1.5 %collective-permute-start.4 = (bf16[16,56,128]{2,1,0:T(8,128)(2,1)S(1)}, bf16[16,56,128]{2,1,0:T(8,128)(2,1)S(1)}, u32[]{:S(2)}, u32[]{:S(2)}) collective-permute-start(bf16[16,56,128]{2,1,0:T(8,128)(2,1)S(1)} %collective-permute-done.3.near_ref), channel_id=1, source_target_pairs={{0,16},{16,0},{32,48},{48,32},{64,80},{80,64},{96,112},{112,96},{1... | collective-permute-start | bytes 688136 | tf_op jit(solution)/shard_map/ppermute | solution.py:260
  36.4 4.8 %collective-permute-start = (bf16[16,40,128]{2,1,0:T(8,128)(2,1)S(1)}, bf16[16,40,128]{2,1,0:T(8,128)(2,1)S(1)}, u32[]{:S(2)}, u32[]{:S(2)}) collective-permute-start(bf16[16,40,128]{2,1,0:T(8,128)(2,1)S(1)} %get-tuple-element.7), channel_id=1, source_target_pairs={{2,4},{4,2},{6,8},{8,6},{10,12},{12,10},{14,30},{30,14},{28,26},{2... | collective-permute-start | bytes 491528 | tf_op jit(solution)/shard_map/ppermute | solution.py:269
  37.1 7.1 %collective-permute-start.1 = (bf16[16,40,128]{2,1,0:T(8,128)(2,1)S(1)}, bf16[16,40,128]{2,1,0:T(8,128)(2,1)S(1)}, u32[]{:S(2)}, u32[]{:S(2)}) collective-permute-start(bf16[16,40,128]{2,1,0:T(8,128)(2,1)S(1)} %get-tuple-element.6), channel_id=1, source_target_pairs={{0,2},{2,0},{4,6},{6,4},{8,10},{10,8},{12,14},{14,12},{30,28},{28,... | collective-permute-start | bytes 491528 | tf_op jit(solution)/shard_map/ppermute | solution.py:270

commit v6 on v5

--- a/solution.py
+++ b/solution.py
@@ -21,7 +21,13 @@
 
 
 def pair_of(level, core, count):
-    return level + core * (count // 2 - 1 - 2 * level)
+    step = (level - 1) % (count // 2)
+    return step + core * (count // 2 - 1 - 2 * step)
+
+
+def level_of(pair, core, count):
+    step = pair + core * (count // 2 - 1 - 2 * pair)
+    return (step + 1) % (count // 2)
 
 
 def pieces(taps):
@@ -33,7 +39,7 @@
     return core, y + core * (x - y), x + core * (y - x)
 
 
-def odd(slab, level):
+def rising(slab, level):
     return lax.rem(slab + level, 2)
 
 
@@ -81,7 +87,7 @@
                         edge = side - half
                         turned = pltpu.roll(column, (spot - edge) % height, 1)
                         edges[half] = jnp.where(lane == spot, turned, edges[half])
-            place = plane + lax.rem(pair, 2) * (1 - 2 * plane)
+            place = plane + (1 - lax.rem(pair, 2)) * (1 - 2 * plane)
             start = pl.multiple_of(place * (block + rows), 8)
             for half, values in enumerate(both(*maps)):
                 send_ref[rank_of(2 * level + half, count), pl.ds(start, block), :] = values.astype(BF16)
@@ -138,25 +144,25 @@
     early = lane < side
     within = lane % side
 
-    is_odd = odd(lax.axis_index("gx"), lax.axis_index("level"))
+    is_rising = rising(lax.axis_index("gx"), lax.axis_index("level"))
 
     def edge_of(ref, start):
         parts = [ref[rank_of(chip, count), start : start + rows, :] for chip in range(count)]
         return jnp.concatenate(parts).astype(F32)
 
     own_edge, outer_edge, inner_edge = edge_of(own_ref, block), edge_of(outer_ref, block), edge_of(inner_ref, 0)
-    low_edge = jnp.where(is_odd == 1, inner_edge, outer_edge)
-    high_edge = jnp.where(is_odd == 1, outer_edge, inner_edge)
+    low_edge = jnp.where(is_rising == 1, inner_edge, outer_edge)
+    high_edge = jnp.where(is_rising == 1, outer_edge, inner_edge)
     edges = (
         pltpu.roll(jnp.where(early, own_edge, low_edge), side, 1),
         own_edge,
         pltpu.roll(jnp.where(early, high_edge, own_edge), side, 1),
     )
     planes = (
-        (3 * is_odd, outer_ref, 0),
-        (1 + is_odd, own_ref, 0),
-        (2 - is_odd, own_ref, block + rows),
-        (3 - 3 * is_odd, inner_ref, rows),
+        (3 * is_rising, outer_ref, 0),
+        (1 + is_rising, own_ref, 0),
+        (2 - is_rising, own_ref, block + rows),
+        (3 - 3 * is_rising, inner_ref, rows),
     )
     for at, ref, start in planes:
         for chip in range(count):
@@ -261,13 +267,13 @@
     swaps = [], []
     for side in range(2):
         chain = [
-            slab * count + 2 * pair_of(pair, slab % 2, count) + side for slab in range(slabs) for pair in range(pairs)
+            slab * count + 2 * level_of(pair, slab % 2, count) + side for slab in range(slabs) for pair in range(pairs)
         ]
         for at, device in enumerate(chain):
             after = chain[(at + 1) % len(chain)]
             swaps[at % 2].extend(((device, after), (after, device)))
-    outer = lax.ppermute(got[:, : block + rows], ("gx", *CH), swaps[1])
-    inner = lax.ppermute(got[:, block:span], ("gx", *CH), swaps[0])
+    outer = lax.ppermute(got[:, : block + rows], ("gx", *CH), swaps[0])
+    inner = lax.ppermute(got[:, block:span], ("gx", *CH), swaps[1])
     forward, backward = pl.pallas_call(
         functools.partial(prepare_kernel, taps=taps),
         out_shape=[jax.ShapeDtypeStruct((3 * channels, 9 * channels), BF16)] * 2,

time: 64 us -> 64 us (level)
  starting transfers between devices: 2.02 us -> 3.92 us
  waiting for transfers between devices: 11.4 us -> 9.6 us
    ppermute x2, starting transfers between devices: 1.25 us -> 3.16 us  [the longest x1 2.93 us: local(): outer = lax.ppermute(got[:, :block + rows], ('gx', *CH), swaps[0])]
    ppermute x2, waiting for transfers between devices: 5.9 us -> 4.26 us  [the longest x1 4.25 us: local(): outer = lax.ppermute(got[:, :block + rows], ('gx', *CH), swaps[0])]
  transfers between devices with their start and end apart: 5 -> 5, of which waited for: 4 -> 2; matrix products, arithmetic and copies ran while one was open for 0% -> 0% of each run, Pallas kernels for 1% -> 1%
where the time goes in v6:
time: 64 us; the launch traced here: 63.6 us
  blocking collectives  44.8 us (70%)
  waiting for transfers between devices  9.6 us (15%)
  Pallas kernels  4.55 us (7%)
  starting transfers between devices  3.92 us (6%)
  between operations  0.68 us (1%)
    all_to_all x1, blocking collectives, local(): got = lax.all_to_all(send, CH[::-1], 0, 0, tiled=True)  28.2 us
    all_to_all x1, blocking collectives, local(): back = lax.all_to_all(result, CH[::-1], 0, 0, tiled=True)  16.6 us
    ppermute x1, waiting for transfers between devices, local(): near_filters = lax.ppermute(own_filters, 'gx', across)  5.34 us
    ppermute x1, waiting for transfers between devices, local(): outer = lax.ppermute(got[:, :block + rows], ('gx', *CH), swaps[0])  4.25 us
    ppermute x1, starting transfers between devices, local(): outer = lax.ppermute(got[:, :block + rows], ('gx', *CH), swaps[0])  2.93 us
    pallas_call x1, Pallas kernels, local(): pl.pallas_call(functools.partial(conv_kernel, depth=depth), out_shape=jax...  1.82 us
    pallas_call x1, Pallas kernels, local(): pl.pallas_call(pack_kernel, out_shape=jax.ShapeDtypeStruct((count, span +...  1.4 us
  transfers between devices with their start and end apart: 5, of which 2 were waited for; matrix products, arithmetic and copies ran while one was open for 0% of the time, Pallas kernels for 1%

profile of v6, /device:TPU:2, one launch (start us, length us, event | category | flops | bytes accessed | tf_op | source)
XLA Modules:
  0.0 63.6 jit_solution(935587748559244943)
XLA Ops:
  0.6 1.4 %pack.1 = bf16[16,128,128]{2,1,0:T(8,128)(2,1)S(1)} custom-call(bf16[8,16,4,128]{3,2,1,0:T(4,128)(2,1)} %act_hbm.1, bf16[8,16,4,128]{3,2,1,0:T(4,128)(2,1)} %grad_hbm.1, bf16[27,8,128]{2,1,0:T(8,128)(2,1)} %bitcast.1), custom_call_target="tpu_custom_call" | custom-call | tf_op jit(solution)/shard_map/pack/pallas_call | solution.py:245
  2.0 28.2 %all_to_all.10 = bf16[16,128,128]{2,1,0:T(8,128)(2,1)S(1)} all-to-all(bf16[16,128,128]{2,1,0:T(8,128)(2,1)S(1)} %pack.1), channel_id=1, replica_groups=mesh['gx'=16,'level'=8,'side'=2] {'side','level'}, dimensions={0} | all-to-all | bytes 1048576 | tf_op jit(solution)/shard_map/all_to_all | solution.py:260
  30.2 0.8 %collective-permute-start.3 = (bf16[16,56,128]{2,1,0:T(8,128)(2,1)S(1)}, bf16[16,56,128]{2,1,0:T(8,128)(2,1)S(1)}, u32[]{:S(2)}, u32[]{:S(2)}) collective-permute-start(bf16[16,56,128]{2,1,0:T(8,128)(2,1)S(1)} %slice.19.own_ref), channel_id=1, source_target_pairs={{0,128},{16,48},{32,160},{48,16},{64,192},{80,112},{96,224},{112,8... | collective-permute-start | bytes 688136 | tf_op jit(solution)/shard_map/ppermute | solution.py:264
  31.0 0.0 collective-permute-start.2
  31.0 5.3 %collective-permute-done.3.near_ref = bf16[16,56,128]{2,1,0:T(8,128)(2,1)S(1)} collective-permute-done((bf16[16,56,128]{2,1,0:T(8,128)(2,1)S(1)}, bf16[16,56,128]{2,1,0:T(8,128)(2,1)S(1)}, u32[]{:S(2)}, u32[]{:S(2)}) %collective-permute-start.3) | collective-permute-done | bytes 229408 | tf_op jit(solution)/shard_map/ppermute | solution.py:264
  36.3 0.0 collective-permute-start.4
  36.4 2.9 %collective-permute-start = (bf16[16,40,128]{2,1,0:T(8,128)(2,1)S(1)}, bf16[16,40,128]{2,1,0:T(8,128)(2,1)S(1)}, u32[]{:S(2)}, u32[]{:S(2)}) collective-permute-start(bf16[16,40,128]{2,1,0:T(8,128)(2,1)S(1)} %get-tuple-element.7), channel_id=1, source_target_pairs={{2,4},{4,2},{6,8},{8,6},{10,12},{12,10},{14,0},{0,14},{16,30},{30,... | collective-permute-start | bytes 491528 | tf_op jit(solution)/shard_map/ppermute | solution.py:275
  39.3 0.2 collective-permute-start.1
  39.6 0.0 collective-permute-done.2.core_ref
  39.6 0.0 collective-permute-done.4.diagonal_ref
  39.6 0.4 prepare.1
  40.0 4.3 %collective-permute-done.outer_ref = bf16[16,40,128]{2,1,0:T(8,128)(2,1)S(1)} collective-permute-done((bf16[16,40,128]{2,1,0:T(8,128)(2,1)S(1)}, bf16[16,40,128]{2,1,0:T(8,128)(2,1)S(1)}, u32[]{:S(2)}, u32[]{:S(2)}) %collective-permute-start) | collective-permute-done | bytes 163872 | tf_op jit(solution)/shard_map/ppermute | solution.py:275
  44.3 0.0 collective-permute-done.1.inner_ref
  44.3 1.8 %conv.1 = bf16[16,64,128]{2,1,0:T(8,128)(2,1)S(1)} custom-call(bf16[16,72,128]{2,1,0:T(8,128)(2,1)S(1)} %slice.16.own_ref, bf16[16,40,128]{2,1,0:T(8,128)(2,1)S(1)} %collective-permute-done.outer_ref, bf16[16,40,128]{2,1,0:T(8,128)(2,1)S(1)} %collective-permute-done.1.inner_ref, bf16[384,1152]{1,0:T(8,128)(2,1)S(1)} %get-tuple-element.4.forward_ref, ...), custom_call_target="tpu_custom_call" | custom-call | tf_op jit(solution)/shard_map/conv/pallas_call | solution.py:287
  46.1 16.6 %all_to_all.11.got_ref = bf16[16,64,128]{2,1,0:T(8,128)(2,1)S(1)} all-to-all(bf16[16,64,128]{2,1,0:T(8,128)(2,1)S(1)} %conv.1), channel_id=1, replica_groups=mesh['gx'=16,'level'=8,'side'=2] {'side','level'}, dimensions={0} | all-to-all | bytes 524288 | tf_op jit(solution)/shard_map/all_to_all | solution.py:300
  62.7 0.9 %unpack.1 = (bf16[8,16,4,128]{3,2,1,0:T(4,128)(2,1)}, bf16[8,16,4,128]{3,2,1,0:T(4,128)(2,1)}) custom-call(bf16[16,64,128]{2,1,0:T(8,128)(2,1)S(1)} %all_to_all.11.got_ref), custom_call_target="tpu_custom_call" | custom-call | tf_op jit(solution)/shard_map/unpack/pallas_call | solution.py:301
  (3 shorter events, 0.1 us)
Async XLA Ops:
  30.2 6.1 %collective-permute-start.3 = (bf16[16,56,128]{2,1,0:T(8,128)(2,1)S(1)}, bf16[16,56,128]{2,1,0:T(8,128)(2,1)S(1)}, u32[]{:S(2)}, u32[]{:S(2)}) collective-permute-start(bf16[16,56,128]{2,1,0:T(8,128)(2,1)S(1)} %slice.19.own_ref), channel_id=1, source_target_pairs={{0,128},{16,48},{32,160},{48,16},{64,192},{80,112},{96,224},{112,8... | collective-permute-start | bytes 688136 | tf_op jit(solution)/shard_map/ppermute | solution.py:264
  31.0 8.6 %collective-permute-start.2 = (bf16[16,56,128]{2,1,0:T(8,128)(2,1)S(1)}, bf16[16,56,128]{2,1,0:T(8,128)(2,1)S(1)}, u32[]{:S(2)}, u32[]{:S(2)}) collective-permute-start(bf16[16,56,128]{2,1,0:T(8,128)(2,1)S(1)} %slice.19.own_ref), channel_id=1, source_target_pairs={{0,16},{16,0},{32,48},{48,32},{64,80},{80,64},{96,112},{112,96},{1... | collective-permute-start | bytes 688136 | tf_op jit(solution)/shard_map/ppermute | solution.py:265
  36.3 3.2 %collective-permute-start.4 = (bf16[16,56,128]{2,1,0:T(8,128)(2,1)S(1)}, bf16[16,56,128]{2,1,0:T(8,128)(2,1)S(1)}, u32[]{:S(2)}, u32[]{:S(2)}) collective-permute-start(bf16[16,56,128]{2,1,0:T(8,128)(2,1)S(1)} %collective-permute-done.3.near_ref), channel_id=1, source_target_pairs={{0,16},{16,0},{32,48},{48,32},{64,80},{80,64},{96,112},{112,96},{1... | collective-permute-start | bytes 688136 | tf_op jit(solution)/shard_map/ppermute | solution.py:266
  36.4 7.9 %collective-permute-start = (bf16[16,40,128]{2,1,0:T(8,128)(2,1)S(1)}, bf16[16,40,128]{2,1,0:T(8,128)(2,1)S(1)}, u32[]{:S(2)}, u32[]{:S(2)}) collective-permute-start(bf16[16,40,128]{2,1,0:T(8,128)(2,1)S(1)} %get-tuple-element.7), channel_id=1, source_target_pairs={{2,4},{4,2},{6,8},{8,6},{10,12},{12,10},{14,0},{0,14},{16,30},{30,... | collective-permute-start | bytes 491528 | tf_op jit(solution)/shard_map/ppermute | solution.py:275
  39.3 5.0 %collective-permute-start.1 = (bf16[16,40,128]{2,1,0:T(8,128)(2,1)S(1)}, bf16[16,40,128]{2,1,0:T(8,128)(2,1)S(1)}, u32[]{:S(2)}, u32[]{:S(2)}) collective-permute-start(bf16[16,40,128]{2,1,0:T(8,128)(2,1)S(1)} %get-tuple-element.6), channel_id=1, source_target_pairs={{4,6},{6,4},{8,10},{10,8},{12,14},{14,12},{0,16},{16,0},{30,28},{2... | collective-permute-start | bytes 491528 | tf_op jit(solution)/shard_map/ppermute | solution.py:276

commit v7 on v5

--- a/solution.py
+++ b/solution.py
@@ -11,7 +11,8 @@
 VMEM = pl.BlockSpec(memory_space=pltpu.VMEM)
 HBM = pl.BlockSpec(memory_space=pltpu.HBM)
 PARAMS = pltpu.CompilerParams(vmem_limit_bytes=16 * 2**20)
-CH = ("level", "side")
+CH = ("upper", "lower", "side")
+ORDER = ("side", "lower", "upper")
 F32 = jnp.float32
 BF16 = jnp.bfloat16
 
@@ -38,7 +39,9 @@
 
 
 def rank_of(chip, count):
-    return chip % 2 * (count // 2) + chip // 2
+    level, side = chip // 2, chip % 2
+    levels = count // 2
+    return side * levels + level % (levels // 2) * 2 + level // (levels // 2)
 
 
 def both(first, second):
@@ -138,7 +141,7 @@
     early = lane < side
     within = lane % side
 
-    is_odd = odd(lax.axis_index("gx"), lax.axis_index("level"))
+    is_odd = odd(lax.axis_index("gx"), lax.axis_index("lower"))
 
     def edge_of(ref, start):
         parts = [ref[rank_of(chip, count), start : start + rows, :] for chip in range(count)]
@@ -251,7 +254,7 @@
         compiler_params=PARAMS,
         name="pack",
     )(*(pltpu.with_memory_space_constraint(x, pltpu.HBM) for x in (activations, out_grad, jnp.swapaxes(conv_weight, 1, 2))))
-    got = lax.all_to_all(send, CH[::-1], 0, 0, tiled=True)
+    got = lax.all_to_all(send, ORDER, 0, 0, tiled=True)
     own, own_filters = got[:, :span], got[:, span:]
     across_core = [(slab, slab ^ 1) for slab in range(slabs)]
     across = [(slab, slab ^ (2 if slab % 2 else 8)) for slab in range(slabs)]
@@ -291,7 +294,7 @@
         compiler_params=PARAMS,
         name="conv",
     )(own, outer, inner, forward, backward)
-    back = lax.all_to_all(result, CH[::-1], 0, 0, tiled=True)
+    back = lax.all_to_all(result, ORDER, 0, 0, tiled=True)
     return pl.pallas_call(
         unpack_kernel,
         out_shape=(jax.ShapeDtypeStruct(activations.shape, BF16), jax.ShapeDtypeStruct(out_grad.shape, BF16)),
@@ -304,7 +307,7 @@
 
 def solution(mesh):
     slabs, count = mesh.shape["gx"], mesh.shape["ch"]
-    mesh = Mesh(mesh.devices.reshape(slabs, count // 2, 2), ("gx", *CH))
+    mesh = Mesh(mesh.devices.reshape(slabs, 2, count // 4, 2), ("gx", *CH))
     return jax.shard_map(
         functools.partial(local, slabs, count),
         mesh=mesh,

time: 64 us -> 65.2 us (1.019)
  starting transfers between devices: 2.02 us -> 4.06 us
  waiting for transfers between devices: 11.4 us -> 9.43 us
  blocking collectives: 44.9 us -> 46.3 us
    ppermute x1, starting transfers between devices: 0.52 us -> 2.56 us  [local(): inner = lax.ppermute(got[:, block:span], ('gx', *CH), swaps[0])]
    ppermute x1, waiting for transfers between devices: 2.93 us -> 1.04 us  [local(): outer = lax.ppermute(got[:, :block + rows], ('gx', *CH), swaps[1])]
    all_to_all x2, blocking collectives: 44.9 us -> 46.3 us  [the longest x1 28.4 us: local(): got = lax.all_to_all(send, ORDER, 0, 0, tiled=True)]
  transfers between devices with their start and end apart: 5 -> 5, of which waited for: 4 -> 3; matrix products, arithmetic and copies ran while one was open for 0% -> 0% of each run, Pallas kernels for 1% -> 1%
where the time goes in v7:
time: 65.2 us; the launch traced here: 65.1 us
  blocking collectives  46.3 us (71%)
  waiting for transfers between devices  9.43 us (14%)
  Pallas kernels  4.55 us (7%)
  starting transfers between devices  4.06 us (6%)
  between operations  0.68 us (1%)
    all_to_all x1, blocking collectives, local(): got = lax.all_to_all(send, ORDER, 0, 0, tiled=True)  28.4 us
    all_to_all x1, blocking collectives, local(): back = lax.all_to_all(result, ORDER, 0, 0, tiled=True)  17.9 us
    ppermute x1, waiting for transfers between devices, local(): near_filters = lax.ppermute(own_filters, 'gx', across)  5.34 us
    ppermute x1, waiting for transfers between devices, local(): inner = lax.ppermute(got[:, block:span], ('gx', *CH), swaps[0])  3.05 us
    ppermute x1, starting transfers between devices, local(): inner = lax.ppermute(got[:, block:span], ('gx', *CH), swaps[0])  2.56 us
    pallas_call x1, Pallas kernels, local(): pl.pallas_call(functools.partial(conv_kernel, depth=depth), out_shape=jax...  1.82 us
    pallas_call x1, Pallas kernels, local(): pl.pallas_call(pack_kernel, out_shape=jax.ShapeDtypeStruct((count, span +...  1.4 us
  transfers between devices with their start and end apart: 5, of which 3 were waited for; matrix products, arithmetic and copies ran while one was open for 0% of the time, Pallas kernels for 1%

profile of v7, /device:TPU:2, one launch (start us, length us, event | category | flops | bytes accessed | tf_op | source)
XLA Modules:
  0.0 65.1 jit_solution(5842564378921336228)
XLA Ops:
  0.6 1.4 %pack.1 = bf16[16,128,128]{2,1,0:T(8,128)(2,1)S(1)} custom-call(bf16[8,16,4,128]{3,2,1,0:T(4,128)(2,1)} %act_hbm.1, bf16[8,16,4,128]{3,2,1,0:T(4,128)(2,1)} %grad_hbm.1, bf16[27,8,128]{2,1,0:T(8,128)(2,1)} %bitcast.1), custom_call_target="tpu_custom_call" | custom-call | tf_op jit(solution)/shard_map/pack/pallas_call | solution.py:242
  2.0 28.4 %all_to_all.10 = bf16[16,128,128]{2,1,0:T(8,128)(2,1)S(1)} all-to-all(bf16[16,128,128]{2,1,0:T(8,128)(2,1)S(1)} %pack.1), channel_id=1, replica_groups=mesh['gx'=16,'upper'=2,'lower'=4,'side'=2] {'side','lower','upper'}, dimensions={0} | all-to-all | bytes 1048576 | tf_op jit(solution)/shard_map/all_to_all | solution.py:257
  30.4 0.8 %collective-permute-start.3 = (bf16[16,56,128]{2,1,0:T(8,128)(2,1)S(1)}, bf16[16,56,128]{2,1,0:T(8,128)(2,1)S(1)}, u32[]{:S(2)}, u32[]{:S(2)}) collective-permute-start(bf16[16,56,128]{2,1,0:T(8,128)(2,1)S(1)} %slice.19.own_ref), channel_id=1, source_target_pairs={{0,128},{16,48},{32,160},{48,16},{64,192},{80,112},{96,224},{112,8... | collective-permute-start | bytes 688136 | tf_op jit(solution)/shard_map/ppermute | solution.py:261
  31.2 0.0 collective-permute-start.2
  31.2 5.3 %collective-permute-done.3.near_ref = bf16[16,56,128]{2,1,0:T(8,128)(2,1)S(1)} collective-permute-done((bf16[16,56,128]{2,1,0:T(8,128)(2,1)S(1)}, bf16[16,56,128]{2,1,0:T(8,128)(2,1)S(1)}, u32[]{:S(2)}, u32[]{:S(2)}) %collective-permute-start.3) | collective-permute-done | bytes 229408 | tf_op jit(solution)/shard_map/ppermute | solution.py:261
  36.5 0.0 collective-permute-start.4
  36.6 0.7 %collective-permute-start = (bf16[16,40,128]{2,1,0:T(8,128)(2,1)S(1)}, bf16[16,40,128]{2,1,0:T(8,128)(2,1)S(1)}, u32[]{:S(2)}, u32[]{:S(2)}) collective-permute-start(bf16[16,40,128]{2,1,0:T(8,128)(2,1)S(1)} %get-tuple-element.7), channel_id=1, source_target_pairs={{2,4},{4,2},{6,8},{8,6},{10,12},{12,10},{14,30},{30,14},{28,26},{2... | collective-permute-start | bytes 491528 | tf_op jit(solution)/shard_map/ppermute | solution.py:272
  37.3 2.6 %collective-permute-start.1 = (bf16[16,40,128]{2,1,0:T(8,128)(2,1)S(1)}, bf16[16,40,128]{2,1,0:T(8,128)(2,1)S(1)}, u32[]{:S(2)}, u32[]{:S(2)}) collective-permute-start(bf16[16,40,128]{2,1,0:T(8,128)(2,1)S(1)} %get-tuple-element.6), channel_id=1, source_target_pairs={{0,2},{2,0},{4,6},{6,4},{8,10},{10,8},{12,14},{14,12},{30,28},{28,... | collective-permute-start | bytes 491528 | tf_op jit(solution)/shard_map/ppermute | solution.py:273
  39.9 0.0 collective-permute-done.2.core_ref
  39.9 0.0 collective-permute-done.4.diagonal_ref
  39.9 0.4 prepare.1
  40.4 1.0 %collective-permute-done.outer_ref = bf16[16,40,128]{2,1,0:T(8,128)(2,1)S(1)} collective-permute-done((bf16[16,40,128]{2,1,0:T(8,128)(2,1)S(1)}, bf16[16,40,128]{2,1,0:T(8,128)(2,1)S(1)}, u32[]{:S(2)}, u32[]{:S(2)}) %collective-permute-start) | collective-permute-done | bytes 163872 | tf_op jit(solution)/shard_map/ppermute | solution.py:272
  41.4 3.0 %collective-permute-done.1.inner_ref = bf16[16,40,128]{2,1,0:T(8,128)(2,1)S(1)} collective-permute-done((bf16[16,40,128]{2,1,0:T(8,128)(2,1)S(1)}, bf16[16,40,128]{2,1,0:T(8,128)(2,1)S(1)}, u32[]{:S(2)}, u32[]{:S(2)}) %collective-permute-start.1) | collective-permute-done | bytes 163872 | tf_op jit(solution)/shard_map/ppermute | solution.py:273
  44.5 1.8 %conv.1 = bf16[16,64,128]{2,1,0:T(8,128)(2,1)S(1)} custom-call(bf16[16,72,128]{2,1,0:T(8,128)(2,1)S(1)} %slice.16.own_ref, bf16[16,40,128]{2,1,0:T(8,128)(2,1)S(1)} %collective-permute-done.outer_ref, bf16[16,40,128]{2,1,0:T(8,128)(2,1)S(1)} %collective-permute-done.1.inner_ref, bf16[384,1152]{1,0:T(8,128)(2,1)S(1)} %get-tuple-element.4.forward_ref, ...), custom_call_target="tpu_custom_call" | custom-call | tf_op jit(solution)/shard_map/conv/pallas_call | solution.py:284
  46.3 17.9 %all_to_all.11.got_ref = bf16[16,64,128]{2,1,0:T(8,128)(2,1)S(1)} all-to-all(bf16[16,64,128]{2,1,0:T(8,128)(2,1)S(1)} %conv.1), channel_id=1, replica_groups=mesh['gx'=16,'upper'=2,'lower'=4,'side'=2] {'side','lower','upper'}, dimensions={0} | all-to-all | bytes 524288 | tf_op jit(solution)/shard_map/all_to_all | solution.py:297
  64.2 0.9 %unpack.1 = (bf16[8,16,4,128]{3,2,1,0:T(4,128)(2,1)}, bf16[8,16,4,128]{3,2,1,0:T(4,128)(2,1)}) custom-call(bf16[16,64,128]{2,1,0:T(8,128)(2,1)S(1)} %all_to_all.11.got_ref), custom_call_target="tpu_custom_call" | custom-call | tf_op jit(solution)/shard_map/unpack/pallas_call | solution.py:298
  (3 shorter events, 0.1 us)
Async XLA Ops:
  30.4 6.1 %collective-permute-start.3 = (bf16[16,56,128]{2,1,0:T(8,128)(2,1)S(1)}, bf16[16,56,128]{2,1,0:T(8,128)(2,1)S(1)}, u32[]{:S(2)}, u32[]{:S(2)}) collective-permute-start(bf16[16,56,128]{2,1,0:T(8,128)(2,1)S(1)} %slice.19.own_ref), channel_id=1, source_target_pairs={{0,128},{16,48},{32,160},{48,16},{64,192},{80,112},{96,224},{112,8... | collective-permute-start | bytes 688136 | tf_op jit(solution)/shard_map/ppermute | solution.py:261
  31.2 8.7 %collective-permute-start.2 = (bf16[16,56,128]{2,1,0:T(8,128)(2,1)S(1)}, bf16[16,56,128]{2,1,0:T(8,128)(2,1)S(1)}, u32[]{:S(2)}, u32[]{:S(2)}) collective-permute-start(bf16[16,56,128]{2,1,0:T(8,128)(2,1)S(1)} %slice.19.own_ref), channel_id=1, source_target_pairs={{0,16},{16,0},{32,48},{48,32},{64,80},{80,64},{96,112},{112,96},{1... | collective-permute-start | bytes 688136 | tf_op jit(solution)/shard_map/ppermute | solution.py:262
  36.5 3.4 %collective-permute-start.4 = (bf16[16,56,128]{2,1,0:T(8,128)(2,1)S(1)}, bf16[16,56,128]{2,1,0:T(8,128)(2,1)S(1)}, u32[]{:S(2)}, u32[]{:S(2)}) collective-permute-start(bf16[16,56,128]{2,1,0:T(8,128)(2,1)S(1)} %collective-permute-done.3.near_ref), channel_id=1, source_target_pairs={{0,16},{16,0},{32,48},{48,32},{64,80},{80,64},{96,112},{112,96},{1... | collective-permute-start | bytes 688136 | tf_op jit(solution)/shard_map/ppermute | solution.py:263
  36.6 4.8 %collective-permute-start = (bf16[16,40,128]{2,1,0:T(8,128)(2,1)S(1)}, bf16[16,40,128]{2,1,0:T(8,128)(2,1)S(1)}, u32[]{:S(2)}, u32[]{:S(2)}) collective-permute-start(bf16[16,40,128]{2,1,0:T(8,128)(2,1)S(1)} %get-tuple-element.7), channel_id=1, source_target_pairs={{2,4},{4,2},{6,8},{8,6},{10,12},{12,10},{14,30},{30,14},{28,26},{2... | collective-permute-start | bytes 491528 | tf_op jit(solution)/shard_map/ppermute | solution.py:272
  37.3 7.1 %collective-permute-start.1 = (bf16[16,40,128]{2,1,0:T(8,128)(2,1)S(1)}, bf16[16,40,128]{2,1,0:T(8,128)(2,1)S(1)}, u32[]{:S(2)}, u32[]{:S(2)}) collective-permute-start(bf16[16,40,128]{2,1,0:T(8,128)(2,1)S(1)} %get-tuple-element.6), channel_id=1, source_target_pairs={{0,2},{2,0},{4,6},{6,4},{8,10},{10,8},{12,14},{14,12},{30,28},{28,... | collective-permute-start | bytes 491528 | tf_op jit(solution)/shard_map/ppermute | solution.py:273

commit v8 on v5

--- a/solution.py
+++ b/solution.py
@@ -122,7 +122,7 @@
 
 
 def conv_kernel(own_ref, outer_ref, inner_ref, forward_ref, backward_ref, send_ref,
-                forward_cells_ref, backward_cells_ref, wide_ref, *, depth):
+                forward_cells_ref, backward_cells_ref, wide_ref, sums_ref, *, depth):
     count, span, height = own_ref.shape
     rows = span // (2 * depth + 1)
     block = rows * depth
@@ -163,12 +163,13 @@
             values = ref[rank_of(chip, count), start : start + block, :].astype(F32)
             wide_ref[at, chip * block : (chip + 1) * block, :] = values
 
-    for c in range(3):
-        for tensor in range(2):
-            direction = 1 - 2 * tensor
+    def gather(tensor):
+        direction = 1 - 2 * tensor
+        cells_ref = cells_refs[tensor]
+        for c in range(3):
             outside = 0 if direction * (c - 1) < 0 else depth - 1
             if c != 1:
-                cells_refs[tensor][3 * c * channels : 3 * (c + 1) * channels, outside * height : (outside + 1) * height] = (
+                cells_ref[3 * c * channels : 3 * (c + 1) * channels, outside * height : (outside + 1) * height] = (
                     jnp.zeros((3 * channels, height), BF16)
                 )
             for a in range(3):
@@ -177,26 +178,27 @@
                 source = within + direction * (c - 1)
                 inside = (within < depth) & (source >= 0) & (source < depth)
                 moved = pltpu.roll(edge, -shift % height, 1)
-                cells_refs[tensor][spot(3 * c + a), depth * height :] = jnp.where(inside, moved, 0.0).astype(BF16)
-    for z in range(depth):
-        pieces = [wide_ref[at, pl.ds(z, channels, stride=depth), :] for at in range(4)]
-        for step in range(3):
-            for tensor, values in enumerate(both_planes(pieces[step], pieces[step + 1], early, side)):
-                direction = 1 - 2 * tensor
+                cells_ref[spot(3 * c + a), depth * height :] = jnp.where(inside, moved, 0.0).astype(BF16)
+        for z in range(depth):
+            pieces = [wide_ref[at, pl.ds(z, channels, stride=depth), :] for at in range(4)]
+            for step in range(3):
+                values = both_planes(pieces[step], pieces[step + 1], early, side)[tensor].astype(BF16)
                 a = 1 + direction * (step - 1)
-                values = values.astype(BF16)
                 for c in range(3):
                     target = z - direction * (c - 1)
                     if 0 <= target < depth:
-                        cells_refs[tensor][spot(3 * c + a), target * height : (target + 1) * height] = values
-
-    for tensor in range(2):
+                        cells_ref[spot(3 * c + a), target * height : (target + 1) * height] = values
+
+    def multiply(tensor):
         direction = 1 - 2 * tensor
-        filters_ref = (forward_ref, backward_ref)[tensor]
-        sums = jnp.dot(filters_ref[...], cells_refs[tensor][:, : depth * height], preferred_element_type=F32)
+        filters_ref, cells_ref = (forward_ref, backward_ref)[tensor], cells_refs[tensor]
+        sums = jnp.dot(filters_ref[...], cells_ref[:, : depth * height], preferred_element_type=F32)
         b = pl.multiple_of((1 + direction - 2 * direction * right) * channels, channels)
-        beyond = jnp.dot(filters_ref[pl.ds(b, channels), :], cells_refs[tensor][:, depth * height :],
-                         preferred_element_type=F32)
+        beyond = jnp.dot(filters_ref[pl.ds(b, channels), :], cells_ref[:, depth * height :], preferred_element_type=F32)
+        return sums, beyond
+
+    def finish(tensor, sums, beyond):
+        direction = 1 - 2 * tensor
         border = jnp.where(right == 1, 0, side - 1)
         for z in range(depth):
             columns = slice(z * height, (z + 1) * height)
@@ -204,10 +206,17 @@
             before = jnp.where(within == 0, 0.0, pltpu.roll(before, 1, 1))
             after = jnp.where(within == side - 1, 0.0, pltpu.roll(after, height - 1, 1))
             extra = jnp.where(within == border, pltpu.roll(beyond, border + (height - z), 1), 0.0)
-            wide_ref[tensor, pl.ds(z, channels, stride=depth), :] = before + middle + after + extra
+            sums_ref[tensor, pl.ds(z, channels, stride=depth), :] = before + middle + after + extra
         for chip in range(count):
-            result = wide_ref[tensor, chip * block : (chip + 1) * block, :].astype(BF16)
+            result = sums_ref[tensor, chip * block : (chip + 1) * block, :].astype(BF16)
             send_ref[rank_of(chip, count), tensor * block : (tensor + 1) * block, :] = result
+
+    gather(0)
+    first = multiply(0)
+    gather(1)
+    second = multiply(1)
+    finish(0, *first)
+    finish(1, *second)
 
 
 def both_planes(first, second, early, side):
@@ -275,7 +284,7 @@
         out_specs=[VMEM, VMEM],
         scratch_shapes=[pltpu.VMEM((4, count, shared, channels), BF16)],
         cost_estimate=pl.CostEstimate(flops=0, bytes_accessed=4 * 2**20, transcendentals=0),
-        compiler_params=PARAMS,
+        compiler_params=pltpu.CompilerParams(vmem_limit_bytes=16 * 2**20),
         name="prepare",
     )(own_filters, core_filters, near_filters, diagonal_filters)
     result = pl.pallas_call(
@@ -287,6 +296,7 @@
             pltpu.VMEM((9 * channels, (depth + 1) * height), BF16),
             pltpu.VMEM((9 * channels, (depth + 1) * height), BF16),
             pltpu.VMEM((4, channels * depth, height), F32),
+            pltpu.VMEM((2, channels * depth, height), F32),
         ],
         compiler_params=PARAMS,
         name="conv",

time: 64 us -> 64 us (level)
  no operation moved by 1% of the time
where the time goes in v8:
time: 64 us; the launch traced here: 63.6 us
  blocking collectives  44.9 us (70%)
  waiting for transfers between devices  11.4 us (18%)
  Pallas kernels  4.51 us (7%)
  starting transfers between devices  2.02 us (3%)
  between operations  0.67 us (1%)
    all_to_all x1, blocking collectives, local(): got = lax.all_to_all(send, CH[::-1], 0, 0, tiled=True)  28.2 us
    all_to_all x1, blocking collectives, local(): back = lax.all_to_all(result, CH[::-1], 0, 0, tiled=True)  16.7 us
    ppermute x1, waiting for transfers between devices, local(): near_filters = lax.ppermute(own_filters, 'gx', across)  5.34 us
    ppermute x1, waiting for transfers between devices, local(): inner = lax.ppermute(got[:, block:span], ('gx', *CH), swaps[0])  2.97 us
    ppermute x1, waiting for transfers between devices, local(): outer = lax.ppermute(got[:, :block + rows], ('gx', *CH), swaps[1])  2.93 us
    pallas_call x1, Pallas kernels, local(): pl.pallas_call(functools.partial(conv_kernel, depth=depth), out_shape=jax...  1.79 us
    pallas_call x1, Pallas kernels, local(): pl.pallas_call(pack_kernel, out_shape=jax.ShapeDtypeStruct((count, span +...  1.4 us
  transfers between devices with their start and end apart: 5, of which 4 were waited for; matrix products, arithmetic and copies ran while one was open for 0% of the time, Pallas kernels for 1%

profile of v8, /device:TPU:2, one launch (start us, length us, event | category | flops | bytes accessed | tf_op | source)
XLA Modules:
  0.0 63.6 jit_solution(3404209639109942174)
XLA Ops:
  0.6 1.4 %pack.1 = bf16[16,128,128]{2,1,0:T(8,128)(2,1)S(1)} custom-call(bf16[8,16,4,128]{3,2,1,0:T(4,128)(2,1)} %act_hbm.1, bf16[8,16,4,128]{3,2,1,0:T(4,128)(2,1)} %grad_hbm.1, bf16[27,8,128]{2,1,0:T(8,128)(2,1)} %bitcast.1), custom_call_target="tpu_custom_call" | custom-call | tf_op jit(solution)/shard_map/pack/pallas_call | solution.py:248
  2.0 28.2 %all_to_all.10 = bf16[16,128,128]{2,1,0:T(8,128)(2,1)S(1)} all-to-all(bf16[16,128,128]{2,1,0:T(8,128)(2,1)S(1)} %pack.1), channel_id=1, replica_groups=mesh['gx'=16,'level'=8,'side'=2] {'side','level'}, dimensions={0} | all-to-all | bytes 1048576 | tf_op jit(solution)/shard_map/all_to_all | solution.py:263
  30.2 0.8 %collective-permute-start.3 = (bf16[16,56,128]{2,1,0:T(8,128)(2,1)S(1)}, bf16[16,56,128]{2,1,0:T(8,128)(2,1)S(1)}, u32[]{:S(2)}, u32[]{:S(2)}) collective-permute-start(bf16[16,56,128]{2,1,0:T(8,128)(2,1)S(1)} %slice.19.own_ref), channel_id=1, source_target_pairs={{0,128},{16,48},{32,160},{48,16},{64,192},{80,112},{96,224},{112,8... | collective-permute-start | bytes 688136 | tf_op jit(solution)/shard_map/ppermute | solution.py:267
  31.0 0.0 collective-permute-start.2
  31.0 5.3 %collective-permute-done.3.near_ref = bf16[16,56,128]{2,1,0:T(8,128)(2,1)S(1)} collective-permute-done((bf16[16,56,128]{2,1,0:T(8,128)(2,1)S(1)}, bf16[16,56,128]{2,1,0:T(8,128)(2,1)S(1)}, u32[]{:S(2)}, u32[]{:S(2)}) %collective-permute-start.3) | collective-permute-done | bytes 229408 | tf_op jit(solution)/shard_map/ppermute | solution.py:267
  36.3 0.0 collective-permute-start.4
  36.4 0.7 %collective-permute-start = (bf16[16,40,128]{2,1,0:T(8,128)(2,1)S(1)}, bf16[16,40,128]{2,1,0:T(8,128)(2,1)S(1)}, u32[]{:S(2)}, u32[]{:S(2)}) collective-permute-start(bf16[16,40,128]{2,1,0:T(8,128)(2,1)S(1)} %get-tuple-element.7), channel_id=1, source_target_pairs={{2,4},{4,2},{6,8},{8,6},{10,12},{12,10},{14,30},{30,14},{28,26},{2... | collective-permute-start | bytes 491528 | tf_op jit(solution)/shard_map/ppermute | solution.py:278
  37.1 0.5 collective-permute-start.1
  37.7 0.0 collective-permute-done.2.core_ref
  37.7 0.2 collective-permute-done.4.diagonal_ref
  37.8 0.4 prepare.1
  38.3 2.9 %collective-permute-done.outer_ref = bf16[16,40,128]{2,1,0:T(8,128)(2,1)S(1)} collective-permute-done((bf16[16,40,128]{2,1,0:T(8,128)(2,1)S(1)}, bf16[16,40,128]{2,1,0:T(8,128)(2,1)S(1)}, u32[]{:S(2)}, u32[]{:S(2)}) %collective-permute-start) | collective-permute-done | bytes 163872 | tf_op jit(solution)/shard_map/ppermute | solution.py:278
  41.2 3.0 %collective-permute-done.1.inner_ref = bf16[16,40,128]{2,1,0:T(8,128)(2,1)S(1)} collective-permute-done((bf16[16,40,128]{2,1,0:T(8,128)(2,1)S(1)}, bf16[16,40,128]{2,1,0:T(8,128)(2,1)S(1)}, u32[]{:S(2)}, u32[]{:S(2)}) %collective-permute-start.1) | collective-permute-done | bytes 163872 | tf_op jit(solution)/shard_map/ppermute | solution.py:279
  44.2 1.8 %conv.1 = bf16[16,64,128]{2,1,0:T(8,128)(2,1)S(1)} custom-call(bf16[16,72,128]{2,1,0:T(8,128)(2,1)S(1)} %slice.16.own_ref, bf16[16,40,128]{2,1,0:T(8,128)(2,1)S(1)} %collective-permute-done.outer_ref, bf16[16,40,128]{2,1,0:T(8,128)(2,1)S(1)} %collective-permute-done.1.inner_ref, bf16[384,1152]{1,0:T(8,128)(2,1)S(1)} %get-tuple-element.4.forward_ref, ...), custom_call_target="tpu_custom_call" | custom-call | tf_op jit(solution)/shard_map/conv/pallas_call | solution.py:290
  46.0 16.7 %all_to_all.11.got_ref = bf16[16,64,128]{2,1,0:T(8,128)(2,1)S(1)} all-to-all(bf16[16,64,128]{2,1,0:T(8,128)(2,1)S(1)} %conv.1), channel_id=1, replica_groups=mesh['gx'=16,'level'=8,'side'=2] {'side','level'}, dimensions={0} | all-to-all | bytes 524288 | tf_op jit(solution)/shard_map/all_to_all | solution.py:304
  62.7 0.9 %unpack.1 = (bf16[8,16,4,128]{3,2,1,0:T(4,128)(2,1)}, bf16[8,16,4,128]{3,2,1,0:T(4,128)(2,1)}) custom-call(bf16[16,64,128]{2,1,0:T(8,128)(2,1)S(1)} %all_to_all.11.got_ref), custom_call_target="tpu_custom_call" | custom-call | tf_op jit(solution)/shard_map/unpack/pallas_call | solution.py:305
  (3 shorter events, 0.1 us)
Async XLA Ops:
  30.2 6.1 %collective-permute-start.3 = (bf16[16,56,128]{2,1,0:T(8,128)(2,1)S(1)}, bf16[16,56,128]{2,1,0:T(8,128)(2,1)S(1)}, u32[]{:S(2)}, u32[]{:S(2)}) collective-permute-start(bf16[16,56,128]{2,1,0:T(8,128)(2,1)S(1)} %slice.19.own_ref), channel_id=1, source_target_pairs={{0,128},{16,48},{32,160},{48,16},{64,192},{80,112},{96,224},{112,8... | collective-permute-start | bytes 688136 | tf_op jit(solution)/shard_map/ppermute | solution.py:267
  31.0 6.7 %collective-permute-start.2 = (bf16[16,56,128]{2,1,0:T(8,128)(2,1)S(1)}, bf16[16,56,128]{2,1,0:T(8,128)(2,1)S(1)}, u32[]{:S(2)}, u32[]{:S(2)}) collective-permute-start(bf16[16,56,128]{2,1,0:T(8,128)(2,1)S(1)} %slice.19.own_ref), channel_id=1, source_target_pairs={{0,16},{16,0},{32,48},{48,32},{64,80},{80,64},{96,112},{112,96},{1... | collective-permute-start | bytes 688136 | tf_op jit(solution)/shard_map/ppermute | solution.py:268
  36.3 1.5 %collective-permute-start.4 = (bf16[16,56,128]{2,1,0:T(8,128)(2,1)S(1)}, bf16[16,56,128]{2,1,0:T(8,128)(2,1)S(1)}, u32[]{:S(2)}, u32[]{:S(2)}) collective-permute-start(bf16[16,56,128]{2,1,0:T(8,128)(2,1)S(1)} %collective-permute-done.3.near_ref), channel_id=1, source_target_pairs={{0,16},{16,0},{32,48},{48,32},{64,80},{80,64},{96,112},{112,96},{1... | collective-permute-start | bytes 688136 | tf_op jit(solution)/shard_map/ppermute | solution.py:269
  36.4 4.8 %collective-permute-start = (bf16[16,40,128]{2,1,0:T(8,128)(2,1)S(1)}, bf16[16,40,128]{2,1,0:T(8,128)(2,1)S(1)}, u32[]{:S(2)}, u32[]{:S(2)}) collective-permute-start(bf16[16,40,128]{2,1,0:T(8,128)(2,1)S(1)} %get-tuple-element.7), channel_id=1, source_target_pairs={{2,4},{4,2},{6,8},{8,6},{10,12},{12,10},{14,30},{30,14},{28,26},{2... | collective-permute-start | bytes 491528 | tf_op jit(solution)/shard_map/ppermute | solution.py:278
  37.1 7.1 %collective-permute-start.1 = (bf16[16,40,128]{2,1,0:T(8,128)(2,1)S(1)}, bf16[16,40,128]{2,1,0:T(8,128)(2,1)S(1)}, u32[]{:S(2)}, u32[]{:S(2)}) collective-permute-start(bf16[16,40,128]{2,1,0:T(8,128)(2,1)S(1)} %get-tuple-element.6), channel_id=1, source_target_pairs={{0,2},{2,0},{4,6},{6,4},{8,10},{10,8},{12,14},{14,12},{30,28},{28,... | collective-permute-start | bytes 491528 | tf_op jit(solution)/shard_map/ppermute | solution.py:279
